TPU v7x, 256 devices: a whole 4x4x8 slice. The times are simulated.
256 devices in a mesh: row: 8 (over x, core), col: 32 (over z, y).
Axes of the slice: x: 4, y: 4, z: 8, core: 2. Of those that a mesh axis runs over, the one named last changes fastest.
Arguments:
- region: bfloat16 [128, 1024, 256], P('row', 'col'), may hold values from -6 to 6
- reduce_weight: bfloat16 [256, 512], P(None, 'col'), may hold values from -0.375 to 0.375
- group_weight: bfloat16 [144, 512], P(None, 'col'), may hold values from -0.5 to 0.5
- expand_weight: bfloat16 [512, 512], P(None, 'col'), may hold values from -0.25 to 0.25
- shortcut_weight: bfloat16 [256, 512], P(None, 'col'), may hold values from -0.375 to 0.375
- cotangent: bfloat16 [64, 512, 512], P('row', 'col'), may hold values from -6 to 6
Outputs:
- block_out: bfloat16 [64, 512, 512], P('row', 'col')
- region_grad: bfloat16 [128, 1024, 256], P('row', 'col')
- reduce_grad: float32 [256, 512], P(None, 'col')
- group_grad: float32 [144, 512], P(None, 'col')
- expand_grad: float32 [512, 512], P(None, 'col')
- shortcut_grad: float32 [256, 512], P(None, 'col')
All inputs are finite; a program needn't handle non-finite values.
Results may differ from a plain program's by a relative error of at most 0.0061.
Values may be sent and summed in bfloat16 or wider, within the bound.
A program may use at most 128 MiB of HBM per device.

v0:
```python
import jax
import jax.numpy as jnp
from jax import lax
from jax.sharding import PartitionSpec as P

GROUPS = 32
GW = 16


def shifted(x, axis, by):
    devices = lax.axis_size(axis)
    pairs = [(i, i + by) for i in range(devices) if 0 <= i + by < devices]
    return lax.ppermute(x, axis, pairs)


def activate(value):
    return value * jax.nn.sigmoid(value)


def slope(value):
    sigma = jax.nn.sigmoid(value)
    return sigma * (1.0 + value * (1.0 - sigma))


def tap_patch(padded, row_step, col_step, half_rows, half_cols):
    width_mid = padded.shape[2]
    patch = lax.slice(
        padded,
        (row_step, col_step, 0),
        (row_step + 2 * half_rows - 1, col_step + 2 * half_cols - 1, width_mid),
        (2, 2, 1),
    )
    return patch.reshape(half_rows, half_cols, GROUPS, GW)


def per_device(region, reduce_weight, group_weight, expand_weight, shortcut_weight, cotangent):
    tile_rows, tile_cols, in_chans = region.shape
    half_rows = tile_rows // 2
    half_cols = tile_cols // 2
    full_reduce, full_group, full_expand, full_short = (
        lax.all_gather(reduce_weight, "col", axis=1, tiled=True),
        lax.all_gather(group_weight, "col", axis=1, tiled=True),
        lax.all_gather(expand_weight, "col", axis=1, tiled=True),
        lax.all_gather(shortcut_weight, "col", axis=1, tiled=True),
    )
    width_mid = full_reduce.shape[1]
    width_out = full_expand.shape[1]
    flat = region.reshape(-1, in_chans)
    pre_one = jnp.dot(flat, full_reduce, preferred_element_type=jnp.float32).reshape(
        tile_rows, tile_cols, width_mid
    )
    hidden_one = activate(pre_one).astype(jnp.bfloat16)
    upper_rim = shifted(hidden_one[-1:], "row", 1)
    extended = jnp.concatenate([upper_rim, hidden_one], axis=0)
    left_rim = shifted(extended[:, -1:], "col", 1)
    padded = jnp.concatenate([left_rim, extended], axis=1)
    patches = []
    kernels = []
    accum = jnp.zeros((GROUPS, half_rows, half_cols, GW), jnp.float32)
    for offset in range(9):
        row_step, col_step = divmod(offset, 3)
        patch = tap_patch(padded, row_step, col_step, half_rows, half_cols)
        kernel = full_group[offset * GW : (offset + 1) * GW].reshape(GW, GROUPS, GW)
        patches.append(patch)
        kernels.append(kernel)
        accum = accum + lax.dot_general(
            patch, kernel, (((3,), (0,)), ((2,), (1,))), preferred_element_type=jnp.float32
        )
    pre_two = jnp.transpose(accum, (1, 2, 0, 3)).reshape(-1, width_mid)
    hidden_two = activate(pre_two).astype(jnp.bfloat16)
    strided = region[::2, ::2].reshape(-1, in_chans)
    summed = jnp.dot(hidden_two, full_expand, preferred_element_type=jnp.float32) + jnp.dot(
        strided, full_short, preferred_element_type=jnp.float32
    )
    block_out = activate(summed).astype(jnp.bfloat16).reshape(half_rows, half_cols, width_out)
    grad_sum = (cotangent.reshape(-1, width_out).astype(jnp.float32) * slope(summed)).astype(
        jnp.bfloat16
    )
    contract_rows = (((0,), (0,)), ((), ()))
    contract_cols = (((1,), (1,)), ((), ()))
    expand_term = lax.dot_general(
        hidden_two, grad_sum, contract_rows, preferred_element_type=jnp.float32
    )
    short_term = lax.dot_general(
        strided, grad_sum, contract_rows, preferred_element_type=jnp.float32
    )
    grad_two = lax.dot_general(
        grad_sum, full_expand, contract_cols, preferred_element_type=jnp.float32
    )
    grad_two = (
        (grad_two * slope(pre_two)).astype(jnp.bfloat16).reshape(half_rows, half_cols, GROUPS, GW)
    )
    spread = jnp.zeros((half_rows + 1, 2, half_cols + 1, 2, width_mid), jnp.float32)
    pieces = []
    for offset in range(9):
        row_step, col_step = divmod(offset, 3)
        piece = lax.dot_general(
            patches[offset],
            grad_two,
            (((0, 1), (0, 1)), ((2,), (2,))),
            preferred_element_type=jnp.float32,
        )
        pieces.append(jnp.transpose(piece, (1, 0, 2)).reshape(GW, width_mid))
        backed = lax.dot_general(
            grad_two,
            kernels[offset],
            (((3,), (2,)), ((2,), (1,))),
            preferred_element_type=jnp.float32,
        )
        backed = jnp.transpose(backed, (1, 2, 0, 3)).reshape(half_rows, half_cols, width_mid)
        row_base = row_step // 2
        col_base = col_step // 2
        spread = spread.at[
            row_base : row_base + half_rows,
            row_step % 2,
            col_base : col_base + half_cols,
            col_step % 2,
        ].add(backed)
    group_term = jnp.concatenate(pieces, axis=0)
    spread = spread.reshape(2 * half_rows + 2, 2 * half_cols + 2, width_mid)[
        : tile_rows + 1, : tile_cols + 1
    ]
    from_right = shifted(spread[:, :1].astype(jnp.bfloat16), "col", -1).astype(jnp.float32)
    folded = spread[:, 1:]
    folded = folded.at[:, -1:].add(from_right)
    from_below = shifted(folded[:1].astype(jnp.bfloat16), "row", -1).astype(jnp.float32)
    folded = folded[1:]
    folded = folded.at[-1:].add(from_below)
    grad_one = (folded * slope(pre_one)).astype(jnp.bfloat16).reshape(-1, width_mid)
    reduce_term = lax.dot_general(flat, grad_one, contract_rows, preferred_element_type=jnp.float32)
    region_grad = lax.dot_general(
        grad_one, full_reduce, contract_cols, preferred_element_type=jnp.float32
    )
    short_back = lax.dot_general(
        grad_sum, full_short, contract_cols, preferred_element_type=jnp.float32
    )
    region_grad = region_grad.reshape(half_rows, 2, half_cols, 2, in_chans)
    region_grad = region_grad.at[:, 0, :, 0].add(short_back.reshape(half_rows, half_cols, in_chans))
    region_grad = region_grad.reshape(tile_rows, tile_cols, in_chans).astype(jnp.bfloat16)
    shards = (
        lax.psum_scatter(reduce_term, "col", scatter_dimension=1, tiled=True),
        lax.psum_scatter(group_term, "col", scatter_dimension=1, tiled=True),
        lax.psum_scatter(expand_term, "col", scatter_dimension=1, tiled=True),
        lax.psum_scatter(short_term, "col", scatter_dimension=1, tiled=True),
    )
    reduce_grad, group_grad, expand_grad, shortcut_grad = lax.psum(
        (shards[0], shards[1], shards[2], shards[3]), "row"
    )
    return (block_out, region_grad, reduce_grad, group_grad, expand_grad, shortcut_grad)


def solution(mesh):
    in_specs = (
        P("row", "col", None),
        P(None, "col"),
        P(None, "col"),
        P(None, "col"),
        P(None, "col"),
        P("row", "col", None),
    )
    out_specs = (
        P("row", "col", None),
        P("row", "col", None),
        P(None, "col"),
        P(None, "col"),
        P(None, "col"),
        P(None, "col"),
    )
    return jax.shard_map(
        per_device, mesh=mesh, in_specs=in_specs, out_specs=out_specs, check_vma=False
    )
```

profile of v0, /device:TPU:1, one launch (start us, length us, event | category | flops | bytes accessed | tf_op | source)
XLA Modules:
  0.0 1276.9 jit_solution(7665294509048165046)
XLA Ops:
  7.2 41.1 %all_gather.12 = bf16[256,512]{0,1:T(8,128)(2,1)S(1)} all-gather(bf16[256,16]{0,1:T(8,128)(2,1)} %param.31), channel_id=1, replica_groups=mesh['row'=8,'col'=32] {'col'}, dimensions={1}, use_global_device_ids=true | all-gather | bytes 270336 | tf_op jit(solution)/shard_map/all_gather | solution.py:41
  50.8 15.9 %collective-permute-start = (bf16[1,32,512]{2,1,0:T(8,128)(2,1)S(1)}, bf16[1,32,512]{2,1,0:T(8,128)(2,1)S(1)}, u32[]{:S(2)}, u32[]{:S(2)}) collective-permute-start(bf16[1,32,512]{2,1,0:T(8,128)(2,1)S(1)} %slice.592), channel_id=1, source_target_pairs={{0,32},{32,64},{64,96},{96,128},{128,160},{160,192},{192,224},{1,3... | collective-permute-start | bytes 98312 | tf_op jit(solution)/shard_map/ppermute | solution.py:13
  71.2 35.8 %all_gather.13 = bf16[144,512]{0,1:T(8,128)(2,1)S(1)} all-gather(bf16[144,16]{0,1:T(8,128)(2,1)S(1)} %copy-done.54), channel_id=1, replica_groups=mesh['row'=8,'col'=32] {'col'}, dimensions={1}, use_global_device_ids=true | all-gather | bytes 152064 | tf_op jit(solution)/shard_map/all_gather | solution.py:42
  107.0 39.0 %all_gather.14 = bf16[512,512]{0,1:T(8,128)(2,1)} all-gather(bf16[512,16]{0,1:T(8,128)(2,1)S(1)} %copy-done.52), channel_id=1, replica_groups=mesh['row'=8,'col'=32] {'col'}, dimensions={1}, use_global_device_ids=true | all-gather | bytes 540672 | tf_op jit(solution)/shard_map/all_gather | solution.py:43
  163.4 40.5 %all_gather.15 = bf16[256,512]{0,1:T(8,128)(2,1)} all-gather(bf16[256,16]{0,1:T(8,128)(2,1)S(1)} %copy-done.55), channel_id=1, replica_groups=mesh['row'=8,'col'=32] {'col'}, dimensions={1}, use_global_device_ids=true | all-gather | bytes 270336 | tf_op jit(solution)/shard_map/all_gather | solution.py:44
  257.7 10.7 reshape.641
  307.5 4.2 copy.168
  311.7 3.7 add.180
  315.3 4.1 copy.171
  319.4 3.7 reshape.642
  323.1 4.2 copy.174
  342.7 4.1 copy.180
  349.9 4.2 copy.183
  357.2 4.2 copy.186
  364.5 4.2 copy.189
  368.6 3.3 reshape.648
  377.3 3.6 collective-permute-done.2
  381.5 38.0 %collective-permute-start.3 = (bf16[1,32,512]{2,1,0:T(8,128)(2,1)S(1)}, bf16[1,32,512]{2,1,0:T(8,128)(2,1)S(1)}, u32[]{:S(2)}, u32[]{:S(2)}) collective-permute-start(bf16[1,32,512]{2,1,0:T(8,128)(2,1)S(1)} %slice.648), channel_id=1, source_target_pairs={{32,0},{64,32},{96,64},{128,96},{160,128},{192,160},{224,192},{33,... | collective-permute-start | bytes 98312 | tf_op jit(solution)/shard_map/ppermute | solution.py:13
  419.6 3.6 collective-permute-done.3
  428.3 120.5 %reduce-scatter.13.cloned.1.call-done = f32[16,144]{1,0:T(8,128)} async-done(((f32[512,144]{1,0:T(8,128)}), f32[16,144]{1,0:T(8,128)}) %reduce-scatter.13.cloned.1.call-update) | async-done | bytes 9232
  550.3 214.2 %reduce-scatter.11.cloned.1.call-done = f32[256,16]{0,1:T(8,128)} async-done(((f32[256,512]{0,1:T(8,128)}), f32[256,16]{0,1:T(8,128)}) %reduce-scatter.11.cloned.1.call-update) | async-done | bytes 16400 | tf_op jit(solution)/shard_map/reduce_scatter | solution.py:144
  764.4 215.4 %reduce-scatter.7.cloned.1.call-done = f32[256,16]{0,1:T(8,128)} async-done(((f32[256,512]{0,1:T(8,128)}), f32[256,16]{0,1:T(8,128)}) %reduce-scatter.7.cloned.1.call-update) | async-done | bytes 16400 | tf_op jit(solution)/shard_map/reduce_scatter | solution.py:141
  979.8 217.0 %reduce-scatter.9.cloned.1.call-done = f32[512,16]{0,1:T(8,128)} async-done(((f32[512,512]{0,1:T(8,128)}), f32[512,16]{0,1:T(8,128)}) %reduce-scatter.9.cloned.1.call-update) | async-done | bytes 32784 | tf_op jit(solution)/shard_map/reduce_scatter | solution.py:143
  1197.9 66.6 %all-reduce.4.cloned.1.call-done = (f32[256,16]{0,1:T(8,128)}, f32[144,16]{1,0:T(8,128)}, f32[512,16]{0,1:T(8,128)}, f32[256,16]{0,1:T(8,128)}) async-done(((f32[256,16]{0,1:T(8,128)}, f32[144,16]{1,0:T(8,128)}, f32[512,16]{0,1:T(8,128)}, f32[256,16]{0,1:T(8,128)}), (f32[256,16]{0,1:T(8,128)}, f32[144,16]{1,0:T(8,128)}, f32[512,16]{0,1:T(8,128)}, f32[256,16]{0,1:T(8,128)})) %all-reduce.4.cloned.1.call-update) | async-done | bytes 74768 | tf_op jit(solution)/shard_map/psum | solution.py:146
  (265 shorter events, 160.4 us)
Async XLA Ops:
  7.2 541.7 %reduce-scatter.13.cloned.1.call-start = ((), (), s32[]{:S(2)}) async-start(), calls=%async_computation.7 | async-start | bytes 540672
  48.3 22.9 %copy-start.54 = (bf16[144,16]{0,1:T(8,128)(2,1)S(1)}, bf16[144,16]{0,1:T(8,128)(2,1)}, u32[]{:S(2)}) copy-start(bf16[144,16]{0,1:T(8,128)(2,1)} %param.32) | copy-start | bytes 13828
  48.3 58.7 %copy-start.52 = (bf16[512,16]{0,1:T(8,128)(2,1)S(1)}, bf16[512,16]{0,1:T(8,128)(2,1)}, u32[]{:S(2)}) copy-start(bf16[512,16]{0,1:T(8,128)(2,1)} %param.33) | copy-start | bytes 49156
  50.8 153.2 %collective-permute-start = (bf16[1,32,512]{2,1,0:T(8,128)(2,1)S(1)}, bf16[1,32,512]{2,1,0:T(8,128)(2,1)S(1)}, u32[]{:S(2)}, u32[]{:S(2)}) collective-permute-start(bf16[1,32,512]{2,1,0:T(8,128)(2,1)S(1)} %slice.592), channel_id=1, source_target_pairs={{0,32},{32,64},{64,96},{96,128},{128,160},{160,192},{192,224},{1,3... | collective-permute-start | bytes 98312 | tf_op jit(solution)/shard_map/ppermute | solution.py:13
  147.1 10.8 copy-start.19
  147.1 12.6 copy-start.23
  147.1 14.4 %copy-start.25 = (bf16[16,512]{0,1:T(8,128)(2,1)}, bf16[16,512]{0,1:T(8,128)(2,1)S(1)}, u32[]{:S(2)}) copy-start(bf16[16,512]{0,1:T(8,128)(2,1)S(1)} %get-tuple-element.172) | copy-start | bytes 49156
  147.1 74.5 %copy-start.29 = (bf16[16,512]{0,1:T(8,128)(2,1)}, bf16[16,512]{0,1:T(8,128)(2,1)S(1)}, u32[]{:S(2)}) copy-start(bf16[16,512]{0,1:T(8,128)(2,1)S(1)} %get-tuple-element.174) | copy-start | bytes 49156
  209.1 7.9 copy-start.42
  209.2 17.5 %collective-permute-start.1 = (bf16[17,1,512]{2,1,0:T(2,128)(2,1)S(1)}, bf16[17,1,512]{2,1,0:T(2,128)(2,1)}, u32[]{:S(2)}, u32[]{:S(2)}) collective-permute-start(bf16[17,1,512]{2,1,0:T(2,128)(2,1)S(1)} %fusion.13), channel_id=1, source_target_pairs={{0,1},{1,2},{2,3},{3,4},{4,5},{5,6},{6,7},{7,8},{8,9},{9,10},{10,1... | collective-permute-start | bytes 52232 | tf_op jit(solution)/shard_map/ppermute | solution.py:13
  242.5 5.7 copy-start.3
  242.5 5.7 copy-start.10
  253.2 15.2 %copy-start.17 = (bf16[8,16,32,16]{1,3,0,2:T(8,128)(2,1)S(1)}, bf16[8,16,32,16]{1,3,0,2:T(8,128)(2,1)}, u32[]{:S(2)}) copy-start(bf16[8,16,32,16]{1,3,0,2:T(8,128)(2,1)} %copy.193) | copy-start | bytes 393220
  257.7 12.2 copy-start.13
  297.9 7.0 copy-start.48
  298.1 7.0 copy-start.47
  299.4 6.0 copy-start.46
  307.1 457.4 %reduce-scatter.11.cloned.1.call-start = ((), (), s32[]{:S(2)}) async-start(), calls=%async_computation.6 | async-start | bytes 540672 | tf_op jit(solution)/shard_map/reduce_scatter | solution.py:144
  373.4 606.4 %reduce-scatter.7.cloned.1.call-start = ((), (), s32[]{:S(2)}) async-start(), calls=%async_computation.4 | async-start | bytes 540672 | tf_op jit(solution)/shard_map/reduce_scatter | solution.py:141
  375.8 5.1 collective-permute-start.2
  381.5 43.3 %copy-start.53 = (bf16[16,32,256]{2,1,0:T(8,128)(2,1)S(1)}, bf16[16,32,256]{2,1,0:T(8,128)(2,1)}, u32[]{:S(2)}) copy-start(bf16[16,32,256]{2,1,0:T(8,128)(2,1)} %param.30) | copy-start | bytes 786436
  381.5 41.7 %collective-permute-start.3 = (bf16[1,32,512]{2,1,0:T(8,128)(2,1)S(1)}, bf16[1,32,512]{2,1,0:T(8,128)(2,1)S(1)}, u32[]{:S(2)}, u32[]{:S(2)}) collective-permute-start(bf16[1,32,512]{2,1,0:T(8,128)(2,1)S(1)} %slice.648), channel_id=1, source_target_pairs={{32,0},{64,32},{96,64},{128,96},{160,128},{192,160},{224,192},{33,... | collective-permute-start | bytes 98312 | tf_op jit(solution)/shard_map/ppermute | solution.py:13
  426.1 770.7 %reduce-scatter.9.cloned.1.call-start = ((), (), s32[]{:S(2)}) async-start(), calls=%async_computation.5 | async-start | bytes 1081344 | tf_op jit(solution)/shard_map/reduce_scatter | solution.py:143
  427.5 837.0 %all-reduce.4.cloned.1.call-start = ((), (), s32[]{:S(2)}) async-start(), calls=%async_computation.8 | async-start | bytes 278528 | tf_op jit(solution)/shard_map/psum | solution.py:146
  (41 other events, 99.2 us)
Sparse Core Ops, SparseCore 0:
  307.2 241.5 reduce-scatter.12
  553.1 211.2 reduce-scatter.10
  768.2 211.4 reduce-scatter.6
  983.9 212.7 reduce-scatter.8
  1199.4 65.1 all-reduce.3
where the time goes:
time: 1280 us
  waiting for transfers between devices  841 us (66%)
  blocking collectives  156 us (12%)
  local copies, waits for them, and re-layouts  146 us (11%)
  starting transfers between devices  58.1 us (5%)
  matrix products  57.1 us (4%)
  between operations  15 us (1%)
    reduce_scatter x1, waiting for transfers between devices, per_device(): lax.psum_scatter(expand_term, 'col', scatter_dimension=1, tiled=True)  217 us
    reduce_scatter x1, waiting for transfers between devices, per_device(): lax.psum_scatter(reduce_term, 'col', scatter_dimension=1, tiled=True)  215 us
    reduce_scatter x1, waiting for transfers between devices, per_device(): lax.psum_scatter(short_term, 'col', scatter_dimension=1, tiled=True)  214 us
    unnamed x6, waiting for transfers between devices  121 us
    psum x1, waiting for transfers between devices, per_device(): lax.psum((shards[0], shards[1], shards[2], shards[3]), 'row')  66.6 us
    ppermute x4, starting transfers between devices, shifted(): return lax.ppermute(x, axis, pairs)  57.4 us
    all_gather x1, blocking collectives, per_device(): lax.all_gather(reduce_weight, 'col', axis=1, tiled=True)  41.1 us
    all_gather x1, blocking collectives, per_device(): lax.all_gather(shortcut_weight, 'col', axis=1, tiled=True)  40.5 us
  transfers between devices with their start and end apart: 9, of which 7 were waited for; matrix products, arithmetic and copies ran while one was open for 9% of the time, Pallas kernels for 0%

commit v1 on v0

v1 whole, which is shorter than its diff:
```python
import functools

import jax
import jax.numpy as jnp
from jax import lax
from jax.experimental import pallas as pl
from jax.experimental.pallas import tpu as pltpu
from jax.sharding import PartitionSpec as P

MESH = pl.DeviceIdType.MESH
BF = jnp.bfloat16
F32 = jnp.float32
NY = 4
GW = 16
LANES = 1280
HALF = LANES // 2
S = 24
PLANE = 256
MO = 224
MW = 192
PW = 48
VMEM = pl.BlockSpec(memory_space=pltpu.VMEM)

NN = (((1,), (0,)), ((), ()))
NT = (((1,), (1,)), ((), ()))


def mm(lhs, rhs, dims):
    return lax.dot_general(lhs, rhs, dims, preferred_element_type=F32)


def sigmoid(value):
    return 0.5 * jnp.tanh(0.5 * value) + 0.5


def remote(src, dst, send_sem, recv_sem, row, col):
    return pltpu.make_async_remote_copy(
        src_ref=src,
        dst_ref=dst,
        send_sem=send_sem,
        recv_sem=recv_sem,
        device_id=(row, col),
        device_id_type=MESH,
    )


def gather_kernel(
    nr, nc, wt, region, cot, full, top, bot, cbot, lft, rgt,
    reg32, cot32, lstrip, fstrip, zs, zr, ys, yr, cs, cr, hs, hr,
):
    nz = nc // NY
    row, col = lax.axis_index("row"), lax.axis_index("col")
    core = lax.rem(row, 2)
    partner = row + 1 - 2 * core
    z, y = col // NY, lax.rem(col, NY)
    lanes = pl.ds(pl.multiple_of(core * HALF, 128), HALF)

    full[z, y] = wt[...]
    for h in range(2):
        side = slice(128 * h, 128 * h + 128)
        for r in range(16):
            reg32[h, 32 * r : 32 * r + 32] = region[r, :, side].astype(F32)
        lstrip[:, side] = reg32[h, pl.ds(31, 16, stride=32), :].astype(BF)
        for q in range(2):
            fstrip[0, :, 256 * q + 128 * h : 256 * q + 128 * h + 128] = reg32[
                h, pl.ds(q, 16, stride=32), :
            ].astype(BF)
    for h in range(4):
        side = slice(128 * h, 128 * h + 128)
        for r in range(8):
            cot32[h, 16 * r : 16 * r + 16] = cot[r, :, side].astype(F32)
        first = cot32[h, pl.ds(0, 8, stride=16), :]
        fstrip[1, :, side] = jnp.concatenate([first, jnp.zeros_like(first)], axis=0).astype(BF)

    has_up, has_down = row > 0, row < nr - 1
    has_left, has_right = col > 0, col < nc - 1

    plan = [
        (has_down, 1, 0, region.at[15], top, 0),
        (has_up, -1, 0, region.at[pl.ds(0, 2)], bot, 1),
        (has_up, -1, 0, cot.at[0], cbot, 2),
    ]
    for k, (there, step) in enumerate(((has_down, 1), (None, 0), (has_up, -1))):
        right = has_right if there is None else has_right & there
        left = has_left if there is None else has_left & there
        plan.append((right, step, 1, lstrip, lft.at[k], 3 + k))
        plan.append((left, step, -1, fstrip, rgt.at[k], 6 + k))
    above = {0: has_up, 1: has_down, 2: has_down}
    for k, there in enumerate((has_up, None, has_down)):
        above[3 + k] = has_left if there is None else has_left & there
        above[6 + k] = has_right if there is None else has_right & there
    zero_of = {0: top, 1: bot, 2: cbot}
    for k in range(3):
        zero_of[3 + k] = lft.at[k]
        zero_of[6 + k] = rgt.at[k]
    for n, ref in zero_of.items():

        @pl.when(jnp.logical_not(above[n]))
        def _(ref=ref):
            ref[...] = jnp.zeros(ref.shape, ref.dtype)

    barrier = pltpu.get_barrier_semaphore()

    def greet(to_row, to_col):
        pl.semaphore_signal(barrier, inc=1, device_id=(to_row, to_col), device_id_type=MESH)

    for d in range(1, nz):
        greet(row, lax.rem(z + d, nz) * NY + y)
    for d in range(1, NY):
        greet(row, z * NY + lax.rem(y + d, NY))
    greet(partner, col)
    count = nz - 1 + NY - 1 + 1
    for dr in (-1, 0, 1):
        for dc in (-1, 0, 1):
            if dr == 0 and dc == 0:
                continue
            there = None
            for step, less, more in ((dr, has_up, has_down), (dc, has_left, has_right)):
                if step:
                    flag = more if step > 0 else less
                    there = flag if there is None else there & flag
            count = count + there.astype(jnp.int32)

            @pl.when(there)
            def _(dr=dr, dc=dc):
                greet(row + dr, col + dc)

    pl.semaphore_wait(barrier, count)

    along_z = []
    for d in range(1, nz):
        copy = remote(
            wt.at[:, lanes], full.at[z, y, :, lanes], zs.at[d], zr.at[d],
            row, lax.rem(z + d, nz) * NY + y,
        )
        copy.start()
        along_z.append(copy)
    halos = []
    for there, dr, dc, src, dst, n in plan:
        copy = remote(src, dst, hs.at[n], hr.at[n], row + dr, col + dc)
        halos.append((there, copy, n))

        @pl.when(there)
        def _(copy=copy):
            copy.start()

    for copy in along_z:
        copy.wait_recv()
    along_y = []
    for d in range(1, NY):
        copy = remote(
            full.at[:, y, :, lanes], full.at[:, y, :, lanes], ys.at[d], yr.at[d],
            row, z * NY + lax.rem(y + d, NY),
        )
        copy.start()
        along_y.append(copy)
    for copy in along_y:
        copy.wait_recv()
    across = remote(full.at[:, :, :, lanes], full.at[:, :, :, lanes], cs, cr, partner, col)
    across.start()
    for there, copy, n in halos:

        @pl.when(there)
        def _(copy=copy):
            copy.wait_send()

        @pl.when(above[n])
        def _(copy=copy):
            copy.wait_recv()

    for copy in along_z + along_y:
        copy.wait_send()
    across.wait()


def gather(nr, nc, wt, region, cot):
    nz = nc // NY
    kw = wt.shape[0]
    shape = jax.ShapeDtypeStruct
    return pl.pallas_call(
        functools.partial(gather_kernel, nr, nc),
        out_shape=(
            shape((nz, NY, kw, LANES), BF),
            shape((32, 256), BF),
            shape((2, 32, 256), BF),
            shape((16, 512), BF),
            shape((3, 16, 256), BF),
            shape((3, 2, 16, 512), BF),
        ),
        in_specs=[VMEM] * 3,
        out_specs=(VMEM,) * 6,
        scratch_shapes=[
            pltpu.VMEM((2, 512, 128), F32),
            pltpu.VMEM((4, 128, 128), F32),
            pltpu.VMEM((16, 256), BF),
            pltpu.VMEM((2, 16, 512), BF),
            pltpu.SemaphoreType.DMA((nz,)),
            pltpu.SemaphoreType.DMA((nz,)),
            pltpu.SemaphoreType.DMA((NY,)),
            pltpu.SemaphoreType.DMA((NY,)),
            pltpu.SemaphoreType.DMA,
            pltpu.SemaphoreType.DMA,
            pltpu.SemaphoreType.DMA((9,)),
            pltpu.SemaphoreType.DMA((9,)),
        ],
        compiler_params=pltpu.CompilerParams(
            collective_id=0, has_side_effects=True, vmem_limit_bytes=24 << 20
        ),
        name="gather",
    )(wt, region, cot)


def tap_source(tap):
    a, b = divmod(tap, 3)
    plane = (a % 2) * 2 + b % 2
    return plane, (a == 2) * S + (b == 2)


def block_kernel(
    region, cot, full, top, bot, cbot, lft, rgt, block_out, region_grad, gt,
    image, xp, hid, sl1, bdt, h2, sl2, c32, gs, gso, g2, gsot, g2ot, g1, g1t, rg,
):
    image[...] = jnp.zeros_like(image)
    for h in range(2):
        side = slice(128 * h, 128 * h + 128)
        for r in range(16):
            image[h, (r + 1) * PW + 1 : (r + 1) * PW + 33] = region[r, :, side].astype(F32)
        image[h, 1:33] = top[:, side].astype(F32)
        for r in range(2):
            image[h, (17 + r) * PW + 1 : (17 + r) * PW + 33] = bot[r, :, side].astype(F32)
        image[h, pl.ds(PW, 16, stride=PW), :] = lft[1, :, side].astype(F32)
        image[h, 0:1] = lft[0, :, side].astype(F32)[15:16]
        below = lft[2, :, side].astype(F32)
        for r in range(2):
            image[h, (17 + r) * PW : (17 + r) * PW + 1] = below[r : r + 1]
        for q in range(2):
            side = slice(256 * q + 128 * h, 256 * q + 128 * h + 128)
            image[h, pl.ds(PW + 33 + q, 16, stride=PW), :] = rgt[1, 0, :, side].astype(F32)
            image[h, 33 + q : 34 + q] = rgt[0, 0, :, side].astype(F32)[15:16]
            corner = rgt[2, 0, :, side].astype(F32)
            for r in range(2):
                low = (17 + r) * PW + 33 + q
                image[h, low : low + 1] = corner[r : r + 1]

    c32[...] = jnp.zeros_like(c32)
    for i in range(8):
        c32[i * S : i * S + 16] = cot[i].astype(F32)
    c32[8 * S : 8 * S + 16] = cbot[...].astype(F32)
    edge = rgt[1, 1].astype(F32)
    for i in range(8):
        c32[i * S + 16 : i * S + 17] = edge[i : i + 1]
    c32[8 * S + 16 : 8 * S + 17] = rgt[2, 1].astype(F32)[0:1]

    for k in range(4):
        pr, pc = divmod(k, 2)
        for i in range(10):
            for h in range(2):
                xp[k, i * S : (i + 1) * S, 128 * h : 128 * h + 128] = image[
                    h, pl.ds((2 * i + pr) * PW + pc, S, stride=2), :
                ]
        xp[k, 10 * S :] = jnp.zeros((PLANE - 10 * S, 256), F32)
        hid[k, 10 * S :] = jnp.zeros((PLANE - 10 * S, 512), F32)
        pixels = xp[k, : 10 * S].astype(BF)
        for n in range(2):
            half = slice(256 * n, 256 * n + 256)
            pre = mm(pixels, full[half, 0:256], NT)
            gate = sigmoid(pre)
            act = pre * gate
            hid[k, : 10 * S, half] = act.astype(BF).astype(F32)
            sl1[k, : 10 * S, half] = gate + act * (1.0 - gate)

    lane = lax.broadcasted_iota(jnp.int32, (16, 128), 1) // GW
    for tap in range(9):
        first = 1024 + 128 * (tap // 8)
        for u in range(4):
            t, v = divmod(u, 2)
            for g in range(8):
                low = u * 128 + g * 16
                piece = full[low : low + 16, first : first + 128].astype(F32)
                turn = ((g - tap % 8) * 16) % 128
                if turn:
                    piece = pltpu.roll(piece, turn, 1)
                piece = jnp.where(lane == g, piece, 0.0).astype(BF)
                low = v * 128 + g * 16
                bdt[tap, t, low : low + 16, v * 128 : v * 128 + 128] = piece
                bdt[tap, t, low : low + 16, (1 - v) * 128 : (1 - v) * 128 + 128] = jnp.zeros(
                    (16, 128), BF
                )

    for t in range(2):
        half = slice(256 * t, 256 * t + 256)
        pre = jnp.zeros((MO, 256), F32)
        for tap in range(9):
            k, off = tap_source(tap)
            pre = pre + mm(hid[k, off : off + MO, half].astype(BF), bdt[tap, t], NT)
        gate = sigmoid(pre)
        act = pre * gate
        h2[:, half] = act.astype(BF)
        sl2[:, half] = gate + act * (1.0 - gate)

    own = lax.rem(lax.broadcasted_iota(jnp.int32, (MW, 256), 0), S) < 16
    strided = xp[3, :MO].astype(BF)
    for n in range(2):
        half = slice(256 * n, 256 * n + 256)
        total = mm(h2[...], full[half, 512:1024], NT) + mm(strided, full[half, 256:512], NT)
        gate = sigmoid(total)
        act = total * gate
        for i in range(8):
            block_out[i, :, half] = act[i * S : i * S + 16].astype(BF)
        grad = c32[:, half] * (gate + act * (1.0 - gate))
        gs[:, half] = grad.astype(BF)
        kept = jnp.where(own, grad[:MW], 0.0)
        gso[:, half] = kept.astype(BF)
        gsot[half, :] = jnp.transpose(kept).astype(BF)

    for t in range(2):
        half = slice(256 * t, 256 * t + 256)
        grad = mm(gs[...], full[:, 512 + 256 * t : 768 + 256 * t], NN) * sl2[:, half]
        g2[:, half] = grad.astype(BF).astype(F32)
        g2ot[half, :] = jnp.transpose(jnp.where(own, grad[:MW], 0.0)).astype(BF)

    for n in range(2):
        half = slice(256 * n, 256 * n + 256)
        gt[half, 256:512] = mm(gsot[half, :], strided[:MW], NN).astype(BF)
        for m in range(2):
            gt[half, 512 + 256 * m : 768 + 256 * m] = mm(
                gsot[half, :], h2[:MW, 256 * m : 256 * m + 256], NN
            ).astype(BF)
    for u in range(4):
        block = slice(128 * u, 128 * u + 128)
        sums = [[jnp.zeros((16, 128), F32)] * 8, [jnp.zeros((16, 128), F32)] * 8]
        for tap in range(9):
            k, off = tap_source(tap)
            outer = mm(g2ot[block, :], hid[k, off : off + MW, block].astype(BF), NN)
            for g in range(8):
                piece = outer[g * 16 : g * 16 + 16]
                turn = ((tap % 8 - g) * 16) % 128
                if turn:
                    piece = pltpu.roll(piece, turn, 1)
                sums[tap // 8][g] = jnp.where(lane == tap % 8, piece, sums[tap // 8][g])
        for h in range(2):
            for g in range(8):
                low = u * 128 + g * 16
                gt[low : low + 16, 1024 + 128 * h : 1152 + 128 * h] = sums[h][g].astype(BF)

    for k in range(4):
        pr, pc = divmod(k, 2)
        window = (1 - pr) * S + (1 - pc)
        for t in range(2):
            half = slice(256 * t, 256 * t + 256)
            spread = jnp.zeros((MW, 256), F32)
            for tap in range(9):
                a, b = divmod(tap, 3)
                if tap_source(tap)[0] != k:
                    continue
                off = (a == 0) * S + (b == 0)
                spread = spread + mm(g2[off : off + MW, half].astype(BF), bdt[tap, t], NN)
            grad = jnp.where(own, spread * sl1[k, window : window + MW, half], 0.0)
            g1[k, :, half] = grad.astype(BF)
            g1t[k, half, :] = jnp.transpose(grad).astype(BF)
        back = mm(g1[k], full[:, 0:256], NN)
        if k == 3:
            back = back + mm(gso[...], full[:, 256:512], NN)
        for i in range(8):
            line = (2 * i + 1 - pr) * 32 + 1 - pc
            for h in range(2):
                rg[h, pl.ds(line, 16, stride=2), :] = back[
                    i * S : i * S + 16, 128 * h : 128 * h + 128
                ]
    for n in range(2):
        half = slice(256 * n, 256 * n + 256)
        grad = jnp.zeros((256, 256), F32)
        for k in range(4):
            pr, pc = divmod(k, 2)
            window = (1 - pr) * S + (1 - pc)
            grad = grad + mm(g1t[k, half, :], xp[k, window : window + MW].astype(BF), NN)
        gt[half, 0:256] = grad.astype(BF)
    for r in range(16):
        for h in range(2):
            region_grad[r, :, 128 * h : 128 * h + 128] = rg[h, 32 * r : 32 * r + 32].astype(BF)


def block(region, cot, full, *halos):
    shape = jax.ShapeDtypeStruct
    return pl.pallas_call(
        block_kernel,
        out_shape=(
            shape((8, 16, 512), BF),
            shape((16, 32, 256), BF),
            shape((512, LANES), BF),
        ),
        in_specs=[VMEM] * 8,
        out_specs=(VMEM,) * 3,
        scratch_shapes=[
            pltpu.VMEM((2, 20 * PW, 128), F32),
            pltpu.VMEM((4, PLANE, 256), F32),
            pltpu.VMEM((4, PLANE, 512), F32),
            pltpu.VMEM((4, PLANE, 512), F32),
            pltpu.VMEM((9, 2, 256, 256), BF),
            pltpu.VMEM((MO, 512), BF),
            pltpu.VMEM((MO, 512), F32),
            pltpu.VMEM((MO, 512), F32),
            pltpu.VMEM((MO, 512), BF),
            pltpu.VMEM((MW, 512), BF),
            pltpu.VMEM((MO, 512), F32),
            pltpu.VMEM((512, MW), BF),
            pltpu.VMEM((512, MW), BF),
            pltpu.VMEM((4, MW, 512), BF),
            pltpu.VMEM((4, 512, MW), BF),
            pltpu.VMEM((2, 512, 128), F32),
        ],
        compiler_params=pltpu.CompilerParams(vmem_limit_bytes=40 << 20),
        name="block",
    )(region, cot, full, *halos)


def reduce_kernel(
    nr, nc, gt, out, rc, s1, ry, s2, rz, rx,
    cs, cr, ys, yr, zs, zr, xs, xr, fs, fr,
):
    nz, nx = nc // NY, nr // 2
    row, col = lax.axis_index("row"), lax.axis_index("col")
    x, core = row // 2, lax.rem(row, 2)
    partner = row + 1 - 2 * core
    z, y = col // NY, lax.rem(col, NY)
    mine = pl.ds(pl.multiple_of(core * HALF, 128), HALF)
    other = pl.ds(pl.multiple_of((1 - core) * HALF, 128), HALF)

    barrier = pltpu.get_barrier_semaphore()

    def greet(to_row, to_col):
        pl.semaphore_signal(barrier, inc=1, device_id=(to_row, to_col), device_id_type=MESH)

    greet(partner, col)
    for d in range(1, NY):
        greet(row, z * NY + lax.rem(y + d, NY))
    for d in range(1, nz):
        greet(row, lax.rem(z + d, nz) * NY + y)
    for d in range(1, nx):
        greet(2 * lax.rem(x + d, nx) + core, col)
    pl.semaphore_wait(barrier, 1 + NY - 1 + nz - 1 + nx - 1)

    across = remote(gt.at[:, :, :, other], rc, cs, cr, partner, col)
    across.start()
    across.wait_recv()

    along_y = []
    for d in range(1, NY):
        to = lax.rem(y + d, NY)
        for n in range(nz):
            s1[n, to] = (gt[n, to, :, mine].astype(F32) + rc[n, to].astype(F32)).astype(BF)
        copy = remote(s1.at[:, to], ry.at[d], ys.at[d], yr.at[d], row, z * NY + to)
        copy.start()
        along_y.append(copy)
    for copy in along_y:
        copy.wait_recv()

    def chip_row(n):
        term = gt[n, y, :, mine].astype(F32) + rc[n, y].astype(F32)
        for d in range(1, NY):
            term = term + ry[d, n].astype(F32)
        return term

    along_z = []
    for d in range(1, nz):
        to = lax.rem(z + d, nz)
        s2[d] = chip_row(to).astype(BF)
        copy = remote(s2.at[d], rz.at[d], zs.at[d], zr.at[d], row, to * NY + y)
        copy.start()
        along_z.append(copy)
    term = chip_row(z)
    for d, copy in enumerate(along_z):
        copy.wait_recv()
        term = term + rz[d + 1].astype(F32)
    rx[x] = term

    along_x = []
    for d in range(1, nx):
        copy = remote(rx.at[x], rx.at[x], xs.at[d], xr.at[d], 2 * lax.rem(x + d, nx) + core, col)
        copy.start()
        along_x.append(copy)
    for copy in along_x:
        copy.wait_recv()
    term = rx[0]
    for n in range(1, nx):
        term = term + rx[n]
    out[:, mine] = term
    final = remote(out.at[:, mine], out.at[:, mine], fs, fr, partner, col)
    final.start()
    final.wait()
    across.wait_send()
    for copy in along_y + along_z + along_x:
        copy.wait_send()


def reduce(nr, nc, gt):
    nz, nx = nc // NY, nr // 2
    kw = gt.shape[2]
    dma = pltpu.SemaphoreType.DMA
    return pl.pallas_call(
        functools.partial(reduce_kernel, nr, nc),
        out_shape=jax.ShapeDtypeStruct((kw, LANES), F32),
        in_specs=[VMEM],
        out_specs=VMEM,
        scratch_shapes=[
            pltpu.VMEM((nz, NY, kw, HALF), BF),
            pltpu.VMEM((nz, NY, kw, HALF), BF),
            pltpu.VMEM((NY, nz, kw, HALF), BF),
            pltpu.VMEM((nz, kw, HALF), BF),
            pltpu.VMEM((nz, kw, HALF), BF),
            pltpu.VMEM((nx, kw, HALF), F32),
            dma, dma, dma((NY,)), dma((NY,)), dma((nz,)), dma((nz,)), dma((nx,)), dma((nx,)), dma, dma,
        ],
        compiler_params=pltpu.CompilerParams(
            collective_id=1, has_side_effects=True, vmem_limit_bytes=24 << 20
        ),
        name="reduce",
    )(gt)


def solution(mesh):
    nr, nc = mesh.shape["row"], mesh.shape["col"]

    def per_device(region, reduce_weight, group_weight, expand_weight, shortcut_weight, cotangent):
        kw = reduce_weight.shape[1]
        blank = jnp.zeros((LANES - 1168, kw), BF)
        wt = jnp.concatenate(
            [reduce_weight, shortcut_weight, expand_weight, group_weight, blank], axis=0
        ).T
        full, *halos = gather(nr, nc, wt, region, cotangent)
        block_out, region_grad, gt = block(region, cotangent, full.reshape(512, LANES), *halos)
        grads = reduce(nr, nc, gt.reshape(nc // NY, NY, kw, LANES)).T
        return (
            block_out, region_grad,
            grads[0:256], grads[1024:1168], grads[512:1024], grads[256:512],
        )

    weight = P(None, "col")
    tile = P("row", "col", None)
    return jax.shard_map(
        per_device,
        mesh=mesh,
        in_specs=(tile, weight, weight, weight, weight, tile),
        out_specs=(tile, tile, weight, weight, weight, weight),
        check_vma=False,
    )
```

time: 1280 us -> 69 us (0.05)
  waiting for transfers between devices: 841 us -> 0 us
  blocking collectives: 156 us -> 0 us
  local copies, waits for them, and re-layouts: 146 us -> 6.38 us
  Pallas kernels: 0 us -> 61.7 us
  starting transfers between devices: 58.1 us -> 0 us
  matrix products: 57.1 us -> 0 us
  between operations: 15 us -> 0.67 us
    reduce_scatter x3 -> x0, waiting for transfers between devices: 646 us -> none  [the longest x1 217 us: per_device(): lax.psum_scatter(expand_term, 'col', scatter_dimension=1, tiled=True)]
    all_gather x4 -> x0, blocking collectives: 156 us -> none  [the longest x1 41.1 us: per_device(): lax.all_gather(reduce_weight, 'col', axis=1, tiled=True)]
    unnamed x6 -> x0, waiting for transfers between devices: 121 us -> none
    psum x1 -> x0, waiting for transfers between devices: 66.6 us -> none  [per_device(): lax.psum((shards[0], shards[1], shards[2], shards[3]), 'row')]
    pallas_call x0 -> x3, Pallas kernels: none -> 61.7 us  [the longest x1 29.5 us: reduce(): pl.pallas_call(functools.partial(reduce_kernel, nr, nc), out_shape=jax.Sh...]
    ppermute x4 -> x0, starting transfers between devices: 57.4 us -> none  [shifted(): return lax.ppermute(x, axis, pairs)]
    dot_general x36 -> x0, matrix products: 57.1 us -> none  [the longest x9 17.4 us: per_device(): lax.dot_general(patch, kernel, (((3,), (0,)), ((2,), (1,))), preferred_el...]
    reshape x30 -> x0, local copies, waits for them, and re-layouts: 51 us -> none  [the longest x18 34.7 us: tap_patch(): return patch.reshape(half_rows, half_cols, GROUPS, GW)]
  transfers between devices with their start and end apart: 9 -> 0, of which waited for: 7 -> 0; matrix products, arithmetic and copies ran while one was open for 9% -> 0% of each run, Pallas kernels for 0% -> 0%
where the time goes in v1:
time: 69 us; the launch traced here: 68.7 us
  Pallas kernels  61.7 us (89%)
  local copies, waits for them, and re-layouts  6.38 us (9%)
    pallas_call x1, Pallas kernels, reduce(): pl.pallas_call(functools.partial(reduce_kernel, nr, nc), out_shape=jax.Sh...  29.5 us
    pallas_call x1, Pallas kernels, gather(): pl.pallas_call(functools.partial(gather_kernel, nr, nc), out_shape=(shape...  26.9 us
    pallas_call x1, Pallas kernels, block(): pl.pallas_call(block_kernel, out_shape=(shape((8, 16, 512), BF), shape((1...  5.23 us
    unnamed x8, local copies, waits for them, and re-layouts  3.7 us

profile of v1, /device:TPU:1, one launch (start us, length us, event | category | flops | bytes accessed | tf_op | source)
XLA Modules:
  0.0 68.7 jit_solution(10417549767561351352)
XLA Ops:
  0.6 0.8 %concatenate.3 = bf16[1280,16]{0,1:T(8,128)(2,1)S(1)} concatenate(bf16[256,16]{0,1:T(8,128)(2,1)} %param.7, bf16[256,16]{0,1:T(8,128)(2,1)} %param.10, bf16[512,16]{0,1:T(8,128)(2,1)} %param.9, bf16[144,16]{0,1:T(8,128)(2,1)} %param.8, bf16[112,16]{0,1:T(8,128)(2,1)S(1)} %broadcast_in_dim.3), dimensions={0} | concatenate | bytes 81920 | tf_op jit(solution)/shard_map/concatenate | solution.py:527
  1.5 0.0 copy-start
  1.5 0.9 %copy-done = bf16[16,32,256]{2,1,0:T(8,128)(2,1)S(1)} copy-done((bf16[16,32,256]{2,1,0:T(8,128)(2,1)S(1)}, bf16[16,32,256]{2,1,0:T(8,128)(2,1)}, u32[]{:S(2)}) %copy-start) | copy-done | bytes 262168
  2.4 0.0 copy-start.2
  2.4 0.9 %copy-done.2 = bf16[8,16,512]{2,1,0:T(8,128)(2,1)S(1)} copy-done((bf16[8,16,512]{2,1,0:T(8,128)(2,1)S(1)}, bf16[8,16,512]{2,1,0:T(8,128)(2,1)}, u32[]{:S(2)}) %copy-start.2) | copy-done | bytes 131096
  3.3 26.9 %gather.1 = (bf16[8,4,16,1280]{3,2,1,0:T(8,128)(2,1)S(1)}, bf16[32,256]{1,0:T(8,128)(2,1)S(1)}, bf16[2,32,256]{2,1,0:T(8,128)(2,1)S(1)}, bf16[16,512]{1,0:T(8,12...) custom-call(bf16[16,1280]{1,0:T(8,128)(2,1)S(1)} %bitcast.9, ...), custom_call_target="tpu_custom_call" | custom-call | tf_op jit(solution)/shard_map/gather/pallas_call | solution.py:180
  30.3 0.0 copy-start.1
  30.3 0.9 %copy-done.1 = bf16[16,32,256]{2,1,0:T(8,128)(2,1)S(1)} copy-done((bf16[16,32,256]{2,1,0:T(8,128)(2,1)S(1)}, bf16[16,32,256]{2,1,0:T(8,128)(2,1)}, u32[]{:S(2)}) %copy-start.1) | copy-done | bytes 262168
  31.2 0.0 copy-start.3
  31.2 0.9 %copy-done.3 = bf16[8,16,512]{2,1,0:T(8,128)(2,1)S(1)} copy-done((bf16[8,16,512]{2,1,0:T(8,128)(2,1)S(1)}, bf16[8,16,512]{2,1,0:T(8,128)(2,1)}, u32[]{:S(2)}) %copy-start.3) | copy-done | bytes 131096
  32.1 5.2 %block.1 = (bf16[8,16,512]{2,1,0:T(8,128)(2,1)}, bf16[16,32,256]{2,1,0:T(8,128)(2,1)}, bf16[512,1280]{1,0:T(8,128)(2,1)S(1)}) custom-call(bf16[16,32,256]{2,1,0:T(8,128)(2,1)S(1)} %copy-done.1, bf16[8,16,512]{2,1,0:T(8,128)(2,1)S(1)} %copy-done.3, bf16[512,1280]{1,0:T(8,128)(2,1)S(1)} %bitcast.5, bf16[32,256]{1,0:T(8,128)(2,1)S(1)} %get-tuple-element.16.top, ...), custom_call_target="tpu_custom_call" | custom-call | tf_op jit(solution)/shard_map/block/pallas_call | solution.py:385
  37.4 29.5 %reduce.1 = f32[16,1280]{1,0:T(8,128)S(1)} custom-call(bf16[8,4,16,1280]{3,2,1,0:T(8,128)(2,1)S(1)} %bitcast.4), custom_call_target="tpu_custom_call" | custom-call | tf_op jit(solution)/shard_map/reduce/pallas_call | solution.py:500
  66.9 0.6 slice.17
  67.5 0.6 slice.18
  68.1 0.6 fusion
  (1 shorter events, 0.0 us)
Async XLA Ops:
  1.5 1.0 %copy-start = (bf16[16,32,256]{2,1,0:T(8,128)(2,1)S(1)}, bf16[16,32,256]{2,1,0:T(8,128)(2,1)}, u32[]{:S(2)}) copy-start(bf16[16,32,256]{2,1,0:T(8,128)(2,1)} %region.3) | copy-start | bytes 786436
  2.4 0.9 %copy-start.2 = (bf16[8,16,512]{2,1,0:T(8,128)(2,1)S(1)}, bf16[8,16,512]{2,1,0:T(8,128)(2,1)}, u32[]{:S(2)}) copy-start(bf16[8,16,512]{2,1,0:T(8,128)(2,1)} %cot.3) | copy-start | bytes 393220
  30.3 1.0 %copy-start.1 = (bf16[16,32,256]{2,1,0:T(8,128)(2,1)S(1)}, bf16[16,32,256]{2,1,0:T(8,128)(2,1)}, u32[]{:S(2)}) copy-start(bf16[16,32,256]{2,1,0:T(8,128)(2,1)} %region.3) | copy-start | bytes 786436
  31.2 0.9 %copy-start.3 = (bf16[8,16,512]{2,1,0:T(8,128)(2,1)S(1)}, bf16[8,16,512]{2,1,0:T(8,128)(2,1)}, u32[]{:S(2)}) copy-start(bf16[8,16,512]{2,1,0:T(8,128)(2,1)} %cot.3) | copy-start | bytes 393220

commit v2 on v1

--- a/solution.py
+++ b/solution.py
@@ -45,40 +45,60 @@
 
 
 def gather_kernel(
-    nr, nc, wt, region, cot, full, top, bot, cbot, lft, rgt,
-    reg32, cot32, lstrip, fstrip, zs, zr, ys, yr, cs, cr, hs, hr,
+    nr, nc, wt, region, cot, full, xp, c32,
+    regv, cotv, image, lstrip, fstrip, top, bot, cbot, lft, rgt,
+    ls, zs, zr, us, ur, ds, dr_, fs, fr, cs, cr, hs, hr,
 ):
     nz = nc // NY
     row, col = lax.axis_index("row"), lax.axis_index("col")
     core = lax.rem(row, 2)
     partner = row + 1 - 2 * core
     z, y = col // NY, lax.rem(col, NY)
+    y_up, y_down, y_far = lax.rem(y + 1, NY), lax.rem(y + NY - 1, NY), lax.rem(y + 2, NY)
     lanes = pl.ds(pl.multiple_of(core * HALF, 128), HALF)
-
-    full[z, y] = wt[...]
-    for h in range(2):
-        side = slice(128 * h, 128 * h + 128)
-        for r in range(16):
-            reg32[h, 32 * r : 32 * r + 32] = region[r, :, side].astype(F32)
-        lstrip[:, side] = reg32[h, pl.ds(31, 16, stride=32), :].astype(BF)
-        for q in range(2):
-            fstrip[0, :, 256 * q + 128 * h : 256 * q + 128 * h + 128] = reg32[
-                h, pl.ds(q, 16, stride=32), :
-            ].astype(BF)
-    for h in range(4):
-        side = slice(128 * h, 128 * h + 128)
-        for r in range(8):
-            cot32[h, 16 * r : 16 * r + 16] = cot[r, :, side].astype(F32)
-        first = cot32[h, pl.ds(0, 8, stride=16), :]
-        fstrip[1, :, side] = jnp.concatenate([first, jnp.zeros_like(first)], axis=0).astype(BF)
-
     has_up, has_down = row > 0, row < nr - 1
     has_left, has_right = col > 0, col < nc - 1
 
+    barrier = pltpu.get_barrier_semaphore()
+
+    def greet(to_row, to_col):
+        pl.semaphore_signal(barrier, inc=1, device_id=(to_row, to_col), device_id_type=MESH)
+
+    for d in range(1, nz):
+        greet(row, lax.rem(z + d, nz) * NY + y)
+    greet(row, z * NY + y_up)
+    greet(row, z * NY + y_down)
+    greet(partner, col)
+    count = nz + 2
+    for dr in (-1, 0, 1):
+        for dc in (-1, 0, 1):
+            if dr == 0 and dc == 0:
+                continue
+            there = None
+            for step, less, more in ((dr, has_up, has_down), (dc, has_left, has_right)):
+                if step:
+                    flag = more if step > 0 else less
+                    there = flag if there is None else there & flag
+            count = count + there.astype(jnp.int32)
+
+            @pl.when(there)
+            def _(dr=dr, dc=dc):
+                greet(row + dr, col + dc)
+
+    loads = [
+        pltpu.make_async_copy(region, regv, ls.at[0]),
+        pltpu.make_async_copy(cot, cotv, ls.at[1]),
+    ]
+    for load in loads:
+        load.start()
+    full[z, y, :, lanes] = wt[:, lanes]
+    image[...] = jnp.zeros_like(image)
+    c32[...] = jnp.zeros_like(c32)
+
     plan = [
-        (has_down, 1, 0, region.at[15], top, 0),
-        (has_up, -1, 0, region.at[pl.ds(0, 2)], bot, 1),
-        (has_up, -1, 0, cot.at[0], cbot, 2),
+        (has_down, 1, 0, regv.at[15], top, 0),
+        (has_up, -1, 0, regv.at[pl.ds(0, 2)], bot, 1),
+        (has_up, -1, 0, cotv.at[0], cbot, 2),
     ]
     for k, (there, step) in enumerate(((has_down, 1), (None, 0), (has_up, -1))):
         right = has_right if there is None else has_right & there
@@ -99,42 +119,48 @@
         def _(ref=ref):
             ref[...] = jnp.zeros(ref.shape, ref.dtype)
 
-    barrier = pltpu.get_barrier_semaphore()
-
-    def greet(to_row, to_col):
-        pl.semaphore_signal(barrier, inc=1, device_id=(to_row, to_col), device_id_type=MESH)
-
-    for d in range(1, nz):
-        greet(row, lax.rem(z + d, nz) * NY + y)
-    for d in range(1, NY):
-        greet(row, z * NY + lax.rem(y + d, NY))
-    greet(partner, col)
-    count = nz - 1 + NY - 1 + 1
-    for dr in (-1, 0, 1):
-        for dc in (-1, 0, 1):
-            if dr == 0 and dc == 0:
-                continue
-            there = None
-            for step, less, more in ((dr, has_up, has_down), (dc, has_left, has_right)):
-                if step:
-                    flag = more if step > 0 else less
-                    there = flag if there is None else there & flag
-            count = count + there.astype(jnp.int32)
-
-            @pl.when(there)
-            def _(dr=dr, dc=dc):
-                greet(row + dr, col + dc)
+    for load in loads:
+        load.wait()
+    for h in range(2):
+        side = slice(128 * h, 128 * h + 128)
+        for r in range(16):
+            image[h, (r + 1) * PW + 1 : (r + 1) * PW + 33] = regv[r, :, side].astype(F32)
+        lstrip[:, side] = image[h, pl.ds(PW + 32, 16, stride=PW), :].astype(BF)
+        for q in range(2):
+            fstrip[0, :, 256 * q + 128 * h : 256 * q + 128 * h + 128] = image[
+                h, pl.ds(PW + 1 + q, 16, stride=PW), :
+            ].astype(BF)
+    for h in range(4):
+        side = slice(128 * h, 128 * h + 128)
+        for i in range(8):
+            c32[h, i * S : i * S + 16] = cotv[i, :, side].astype(F32)
+        first = c32[h, pl.ds(0, 8, stride=S), :]
+        fstrip[1, :, side] = jnp.concatenate([first, jnp.zeros_like(first)], axis=0).astype(BF)
 
     pl.semaphore_wait(barrier, count)
 
-    along_z = []
-    for d in range(1, nz):
+    order = [1, nz - 1] if nz > 2 else [1]
+    for d in range(2, nz // 2 + 1):
+        order += [d, nz - d] if d < nz - d else [d]
+    sent = []
+    along_z = {}
+    for d in order:
         copy = remote(
             wt.at[:, lanes], full.at[z, y, :, lanes], zs.at[d], zr.at[d],
             row, lax.rem(z + d, nz) * NY + y,
         )
         copy.start()
-        along_z.append(copy)
+        along_z[d] = copy
+    upward, downward = {}, {}
+
+    def to_neighbours(d):
+        here = full.at[lax.rem(z + nz - d, nz), y, :, lanes]
+        upward[d] = remote(here, here, us.at[d], ur.at[d], row, z * NY + y_up)
+        downward[d] = remote(here, here, ds.at[d], dr_.at[d], row, z * NY + y_down)
+        upward[d].start()
+        downward[d].start()
+
+    to_neighbours(0)
     halos = []
     for there, dr, dc, src, dst, n in plan:
         copy = remote(src, dst, hs.at[n], hr.at[n], row + dr, col + dc)
@@ -144,87 +170,42 @@
         def _(copy=copy):
             copy.start()
 
-    for copy in along_z:
-        copy.wait_recv()
-    along_y = []
-    for d in range(1, NY):
-        copy = remote(
-            full.at[:, y, :, lanes], full.at[:, y, :, lanes], ys.at[d], yr.at[d],
-            row, z * NY + lax.rem(y + d, NY),
-        )
+    for d in order:
+        along_z[d].wait_recv()
+        to_neighbours(d)
+
+    def column(at, n):
+        block = full.at[:, at, :, lanes]
+        copy = remote(block, block, cs.at[n], cr.at[n], partner, col)
         copy.start()
-        along_y.append(copy)
-    for copy in along_y:
-        copy.wait_recv()
-    across = remote(full.at[:, :, :, lanes], full.at[:, :, :, lanes], cs, cr, partner, col)
-    across.start()
+        sent.append(copy)
+
+    column(y, 0)
+
+    forward = {}
+    for d in [0] + order:
+        b = lax.rem(z + nz - d, nz)
+        upward[d].wait_recv()
+        if 2 * d < nz:
+            here = full.at[b, y_down, :, lanes]
+            forward[d] = remote(here, here, fs.at[d], fr.at[d], row, z * NY + y_up)
+            forward[d].start()
+        downward[d].wait_recv()
+        if 2 * d >= nz:
+            here = full.at[b, y_up, :, lanes]
+            forward[d] = remote(here, here, fs.at[d], fr.at[d], row, z * NY + y_down)
+            forward[d].start()
+    column(y_up, 1)
+    column(y_down, 2)
+
     for there, copy, n in halos:
-
-        @pl.when(there)
-        def _(copy=copy):
-            copy.wait_send()
 
         @pl.when(above[n])
         def _(copy=copy):
             copy.wait_recv()
 
-    for copy in along_z + along_y:
-        copy.wait_send()
-    across.wait()
-
-
-def gather(nr, nc, wt, region, cot):
-    nz = nc // NY
-    kw = wt.shape[0]
-    shape = jax.ShapeDtypeStruct
-    return pl.pallas_call(
-        functools.partial(gather_kernel, nr, nc),
-        out_shape=(
-            shape((nz, NY, kw, LANES), BF),
-            shape((32, 256), BF),
-            shape((2, 32, 256), BF),
-            shape((16, 512), BF),
-            shape((3, 16, 256), BF),
-            shape((3, 2, 16, 512), BF),
-        ),
-        in_specs=[VMEM] * 3,
-        out_specs=(VMEM,) * 6,
-        scratch_shapes=[
-            pltpu.VMEM((2, 512, 128), F32),
-            pltpu.VMEM((4, 128, 128), F32),
-            pltpu.VMEM((16, 256), BF),
-            pltpu.VMEM((2, 16, 512), BF),
-            pltpu.SemaphoreType.DMA((nz,)),
-            pltpu.SemaphoreType.DMA((nz,)),
-            pltpu.SemaphoreType.DMA((NY,)),
-            pltpu.SemaphoreType.DMA((NY,)),
-            pltpu.SemaphoreType.DMA,
-            pltpu.SemaphoreType.DMA,
-            pltpu.SemaphoreType.DMA((9,)),
-            pltpu.SemaphoreType.DMA((9,)),
-        ],
-        compiler_params=pltpu.CompilerParams(
-            collective_id=0, has_side_effects=True, vmem_limit_bytes=24 << 20
-        ),
-        name="gather",
-    )(wt, region, cot)
-
-
-def tap_source(tap):
-    a, b = divmod(tap, 3)
-    plane = (a % 2) * 2 + b % 2
-    return plane, (a == 2) * S + (b == 2)
-
-
-def block_kernel(
-    region, cot, full, top, bot, cbot, lft, rgt, block_out, region_grad, gt,
-    image, xp, hid, sl1, bdt, h2, sl2, c32, gs, gso, g2, gsot, g2ot, g1, g1t, rg,
-):
-    image[...] = jnp.zeros_like(image)
     for h in range(2):
         side = slice(128 * h, 128 * h + 128)
-        for r in range(16):
-            image[h, (r + 1) * PW + 1 : (r + 1) * PW + 33] = region[r, :, side].astype(F32)
         image[h, 1:33] = top[:, side].astype(F32)
         for r in range(2):
             image[h, (17 + r) * PW + 1 : (17 + r) * PW + 33] = bot[r, :, side].astype(F32)
@@ -241,16 +222,11 @@
             for r in range(2):
                 low = (17 + r) * PW + 33 + q
                 image[h, low : low + 1] = corner[r : r + 1]
-
-    c32[...] = jnp.zeros_like(c32)
-    for i in range(8):
-        c32[i * S : i * S + 16] = cot[i].astype(F32)
-    c32[8 * S : 8 * S + 16] = cbot[...].astype(F32)
-    edge = rgt[1, 1].astype(F32)
-    for i in range(8):
-        c32[i * S + 16 : i * S + 17] = edge[i : i + 1]
-    c32[8 * S + 16 : 8 * S + 17] = rgt[2, 1].astype(F32)[0:1]
-
+    for h in range(4):
+        side = slice(128 * h, 128 * h + 128)
+        c32[h, 8 * S : 8 * S + 16] = cbot[:, side].astype(F32)
+        c32[h, pl.ds(16, 8, stride=S), :] = rgt[1, 1, :, side].astype(F32)[0:8]
+        c32[h, 8 * S + 16 : 8 * S + 17] = rgt[2, 1, :, side].astype(F32)[0:1]
     for k in range(4):
         pr, pc = divmod(k, 2)
         for i in range(10):
@@ -258,9 +234,77 @@
                 xp[k, i * S : (i + 1) * S, 128 * h : 128 * h + 128] = image[
                     h, pl.ds((2 * i + pr) * PW + pc, S, stride=2), :
                 ]
-        xp[k, 10 * S :] = jnp.zeros((PLANE - 10 * S, 256), F32)
+
+    for d in [0] + order:
+        forward[d].wait_recv()
+    column(y_far, 3)
+    for there, copy, n in halos:
+
+        @pl.when(there)
+        def _(copy=copy):
+            copy.wait_send()
+
+    for group in (along_z, upward, downward, forward):
+        for copy in group.values():
+            copy.wait_send()
+    for copy in sent:
+        copy.wait()
+
+
+def gather(nr, nc, wt, region, cot):
+    nz = nc // NY
+    kw = wt.shape[0]
+    shape = jax.ShapeDtypeStruct
+    hbm = pl.BlockSpec(memory_space=pltpu.HBM)
+    dma = pltpu.SemaphoreType.DMA
+    return pl.pallas_call(
+        functools.partial(gather_kernel, nr, nc),
+        out_shape=(
+            shape((nz, NY, kw, LANES), BF),
+            shape((4, 10 * S, 256), F32),
+            shape((4, MO, 128), F32),
+        ),
+        in_specs=[VMEM, hbm, hbm],
+        out_specs=(VMEM,) * 3,
+        scratch_shapes=[
+            pltpu.VMEM((16, 32, 256), BF),
+            pltpu.VMEM((8, 16, 512), BF),
+            pltpu.VMEM((2, 20 * PW, 128), F32),
+            pltpu.VMEM((16, 256), BF),
+            pltpu.VMEM((2, 16, 512), BF),
+            pltpu.VMEM((32, 256), BF),
+            pltpu.VMEM((2, 32, 256), BF),
+            pltpu.VMEM((16, 512), BF),
+            pltpu.VMEM((3, 16, 256), BF),
+            pltpu.VMEM((3, 2, 16, 512), BF),
+            dma((2,)),
+            dma((nz,)), dma((nz,)),
+            dma((nz,)), dma((nz,)),
+            dma((nz,)), dma((nz,)),
+            dma((nz,)), dma((nz,)),
+            dma((4,)), dma((4,)),
+            dma((9,)), dma((9,)),
+        ],
+        compiler_params=pltpu.CompilerParams(
+            collective_id=0, has_side_effects=True, vmem_limit_bytes=24 << 20
+        ),
+        name="gather",
+    )(wt, region, cot)
+
+
+def tap_source(tap):
+    a, b = divmod(tap, 3)
+    plane = (a % 2) * 2 + b % 2
+    return plane, (a == 2) * S + (b == 2)
+
+
+def block_kernel(
+    full, xp, c32, block_out, region_grad, gt,
+    hid, sl1, bdt, h2, sl2, gs, gso, g2, gsot, g2ot, g1, g1t, rg,
+):
+    for k in range(4):
         hid[k, 10 * S :] = jnp.zeros((PLANE - 10 * S, 512), F32)
-        pixels = xp[k, : 10 * S].astype(BF)
+        pixels = xp[k].astype(BF)
         for n in range(2):
             half = slice(256 * n, 256 * n + 256)
             pre = mm(pixels, full[half, 0:256], NT)
@@ -307,7 +351,8 @@
         act = total * gate
         for i in range(8):
             block_out[i, :, half] = act[i * S : i * S + 16].astype(BF)
-        grad = c32[:, half] * (gate + act * (1.0 - gate))
+        cots = jnp.concatenate([c32[2 * n], c32[2 * n + 1]], axis=1)
+        grad = cots * (gate + act * (1.0 - gate))
         gs[:, half] = grad.astype(BF)
         kept = jnp.where(own, grad[:MW], 0.0)
         gso[:, half] = kept.astype(BF)
@@ -380,7 +425,7 @@
             region_grad[r, :, 128 * h : 128 * h + 128] = rg[h, 32 * r : 32 * r + 32].astype(BF)
 
 
-def block(region, cot, full, *halos):
+def block(full, xp, c32):
     shape = jax.ShapeDtypeStruct
     return pl.pallas_call(
         block_kernel,
@@ -389,16 +434,13 @@
             shape((16, 32, 256), BF),
             shape((512, LANES), BF),
         ),
-        in_specs=[VMEM] * 8,
+        in_specs=[VMEM] * 3,
         out_specs=(VMEM,) * 3,
         scratch_shapes=[
-            pltpu.VMEM((2, 20 * PW, 128), F32),
-            pltpu.VMEM((4, PLANE, 256), F32),
             pltpu.VMEM((4, PLANE, 512), F32),
             pltpu.VMEM((4, PLANE, 512), F32),
             pltpu.VMEM((9, 2, 256, 256), BF),
             pltpu.VMEM((MO, 512), BF),
-            pltpu.VMEM((MO, 512), F32),
             pltpu.VMEM((MO, 512), F32),
             pltpu.VMEM((MO, 512), BF),
             pltpu.VMEM((MW, 512), BF),
@@ -411,18 +453,20 @@
         ],
         compiler_params=pltpu.CompilerParams(vmem_limit_bytes=40 << 20),
         name="block",
-    )(region, cot, full, *halos)
+    )(full, xp, c32)
 
 
 def reduce_kernel(
-    nr, nc, gt, out, rc, s1, ry, s2, rz, rx,
+    nr, nc, gt, out, rc, send, land, s2, rz, rx,
     cs, cr, ys, yr, zs, zr, xs, xr, fs, fr,
 ):
     nz, nx = nc // NY, nr // 2
+    nh = nz // 2
     row, col = lax.axis_index("row"), lax.axis_index("col")
     x, core = row // 2, lax.rem(row, 2)
     partner = row + 1 - 2 * core
     z, y = col // NY, lax.rem(col, NY)
+    y_up, y_down, y_far = lax.rem(y + 1, NY), lax.rem(y + NY - 1, NY), lax.rem(y + 2, NY)
     mine = pl.ds(pl.multiple_of(core * HALF, 128), HALF)
     other = pl.ds(pl.multiple_of((1 - core) * HALF, 128), HALF)
 
@@ -432,46 +476,72 @@
         pl.semaphore_signal(barrier, inc=1, device_id=(to_row, to_col), device_id_type=MESH)
 
     greet(partner, col)
-    for d in range(1, NY):
-        greet(row, z * NY + lax.rem(y + d, NY))
+    greet(row, z * NY + y_up)
+    greet(row, z * NY + y_down)
     for d in range(1, nz):
         greet(row, lax.rem(z + d, nz) * NY + y)
     for d in range(1, nx):
         greet(2 * lax.rem(x + d, nx) + core, col)
-    pl.semaphore_wait(barrier, 1 + NY - 1 + nz - 1 + nx - 1)
-
-    across = remote(gt.at[:, :, :, other], rc, cs, cr, partner, col)
-    across.start()
-    across.wait_recv()
-
-    along_y = []
-    for d in range(1, NY):
-        to = lax.rem(y + d, NY)
-        for n in range(nz):
-            s1[n, to] = (gt[n, to, :, mine].astype(F32) + rc[n, to].astype(F32)).astype(BF)
-        copy = remote(s1.at[:, to], ry.at[d], ys.at[d], yr.at[d], row, z * NY + to)
+    pl.semaphore_wait(barrier, 3 + nz - 1 + nx - 1)
+
+    across = []
+    for n, at in enumerate((y_far, y_up, y_down, y)):
+        copy = remote(gt.at[:, at, :, other], rc.at[:, at], cs.at[n], cr.at[n], partner, col)
         copy.start()
-        along_y.append(copy)
-    for copy in along_y:
-        copy.wait_recv()
-
-    def chip_row(n):
-        term = gt[n, y, :, mine].astype(F32) + rc[n, y].astype(F32)
-        for d in range(1, NY):
-            term = term + ry[d, n].astype(F32)
-        return term
-
-    along_z = []
+        across.append(copy)
+
+    def chip(n, at):
+        return gt[n, at, :, mine].astype(F32) + rc[n, at].astype(F32)
+
+    along_y = {}
+
+    def start_y(n, to):
+        copy = remote(send.at[n], land.at[n], ys.at[n], yr.at[n], row, z * NY + to)
+        copy.start()
+        along_y[n] = copy
+
+    across[0].wait_recv()
+    for k in range(nh):
+        send[0, k] = chip(k, y_far).astype(BF)
+    start_y(0, y_up)
+    for k in range(nh):
+        send[1, k] = chip(nh + k, y_far).astype(BF)
+    start_y(1, y_down)
+    across[1].wait_recv()
+    for k in range(nh):
+        send[2, k] = chip(nh + k, y_up).astype(BF)
+    start_y(2, y_up)
+    across[2].wait_recv()
+    for k in range(nh):
+        send[3, k] = chip(k, y_down).astype(BF)
+    start_y(3, y_down)
+    along_y[0].wait_recv()
+    for k in range(nh):
+        send[4, k] = (chip(k, y_up) + land[0, k].astype(F32)).astype(BF)
+    start_y(4, y_up)
+    along_y[1].wait_recv()
+    for k in range(nh):
+        send[5, k] = (chip(nh + k, y_down) + land[1, k].astype(F32)).astype(BF)
+    start_y(5, y_down)
+    across[3].wait_recv()
+    for n in (2, 3, 4, 5):
+        along_y[n].wait_recv()
+    for k in range(nh):
+        s2[k] = chip(k, y) + land[3, k].astype(F32) + land[4, k].astype(F32)
+        s2[nh + k] = chip(nh + k, y) + land[2, k].astype(F32) + land[5, k].astype(F32)
+
+    along_z = {}
+    order = [nz // 2] + [n for d in range(nz // 2 - 1, 0, -1) for n in (d, nz - d)]
+    for d in order:
+        to = lax.rem(z + d, nz)
+        rz[0, d] = s2[to].astype(BF)
+        copy = remote(rz.at[0, d], rz.at[1, d], zs.at[d], zr.at[d], row, to * NY + y)
+        copy.start()
+        along_z[d] = copy
+    term = s2[z]
     for d in range(1, nz):
-        to = lax.rem(z + d, nz)
-        s2[d] = chip_row(to).astype(BF)
-        copy = remote(s2.at[d], rz.at[d], zs.at[d], zr.at[d], row, to * NY + y)
-        copy.start()
-        along_z.append(copy)
-    term = chip_row(z)
-    for d, copy in enumerate(along_z):
-        copy.wait_recv()
-        term = term + rz[d + 1].astype(F32)
+        along_z[d].wait_recv()
+        term = term + rz[1, d].astype(F32)
     rx[x] = term
 
     along_x = []
@@ -487,10 +557,9 @@
     out[:, mine] = term
     final = remote(out.at[:, mine], out.at[:, mine], fs, fr, partner, col)
     final.start()
+    for copy in across + list(along_y.values()) + list(along_z.values()) + along_x:
+        copy.wait_send()
     final.wait()
-    across.wait_send()
-    for copy in along_y + along_z + along_x:
-        copy.wait_send()
 
 
 def reduce(nr, nc, gt):
@@ -504,12 +573,12 @@
         out_specs=VMEM,
         scratch_shapes=[
             pltpu.VMEM((nz, NY, kw, HALF), BF),
-            pltpu.VMEM((nz, NY, kw, HALF), BF),
-            pltpu.VMEM((NY, nz, kw, HALF), BF),
-            pltpu.VMEM((nz, kw, HALF), BF),
-            pltpu.VMEM((nz, kw, HALF), BF),
+            pltpu.VMEM((6, nz // 2, kw, HALF), BF),
+            pltpu.VMEM((6, nz // 2, kw, HALF), BF),
+            pltpu.VMEM((nz, kw, HALF), F32),
+            pltpu.VMEM((2, nz, kw, HALF), BF),
             pltpu.VMEM((nx, kw, HALF), F32),
-            dma, dma, dma((NY,)), dma((NY,)), dma((nz,)), dma((nz,)), dma((nx,)), dma((nx,)), dma, dma,
+            dma((4,)), dma((4,)), dma((6,)), dma((6,)), dma((nz,)), dma((nz,)), dma((nx,)), dma((nx,)), dma, dma,
         ],
         compiler_params=pltpu.CompilerParams(
             collective_id=1, has_side_effects=True, vmem_limit_bytes=24 << 20
@@ -518,6 +587,24 @@
     )(gt)
 
 
+def split_kernel(slab, reduce_grad, group_grad, expand_grad, shortcut_grad):
+    reduce_grad[...] = slab[:, 0:256]
+    shortcut_grad[...] = slab[:, 256:512]
+    expand_grad[...] = slab[:, 512:1024]
+    group_grad[...] = slab[:, 1024:1168]
+
+
+def split(slab):
+    kw = slab.shape[0]
+    return pl.pallas_call(
+        split_kernel,
+        out_shape=tuple(jax.ShapeDtypeStruct((kw, n), F32) for n in (256, 144, 512, 256)),
+        in_specs=[VMEM],
+        out_specs=(VMEM,) * 4,
+        name="split",
+    )(slab)
+
+
 def solution(mesh):
     nr, nc = mesh.shape["row"], mesh.shape["col"]
 
@@ -527,13 +614,10 @@
         wt = jnp.concatenate(
             [reduce_weight, shortcut_weight, expand_weight, group_weight, blank], axis=0
         ).T
-        full, *halos = gather(nr, nc, wt, region, cotangent)
-        block_out, region_grad, gt = block(region, cotangent, full.reshape(512, LANES), *halos)
-        grads = reduce(nr, nc, gt.reshape(nc // NY, NY, kw, LANES)).T
-        return (
-            block_out, region_grad,
-            grads[0:256], grads[1024:1168], grads[512:1024], grads[256:512],
-        )
+        full, xp, c32 = gather(nr, nc, wt, region, cotangent)
+        block_out, region_grad, gt = block(full.reshape(512, LANES), xp, c32)
+        grads = split(reduce(nr, nc, gt.reshape(nc // NY, NY, kw, LANES)))
+        return (block_out, region_grad, *(grad.T for grad in grads))
 
     weight = P(None, "col")
     tile = P("row", "col", None)

time: 69 us -> 60.2 us (0.87)
  Pallas kernels: 61.7 us -> 56 us
  local copies, waits for them, and re-layouts: 6.38 us -> 3.32 us
    pallas_call x1, Pallas kernels: 29.5 us -> 24.8 us  [reduce(): pl.pallas_call(functools.partial(reduce_kernel, nr, nc), out_shape=jax.Sh...]
    pallas_call x1, Pallas kernels: 26.9 us -> 24.6 us  [gather(): pl.pallas_call(functools.partial(gather_kernel, nr, nc), out_shape=(shape...]
    slice x3 -> x0, local copies, waits for them, and re-layouts: 1.84 us -> none  [the longest x1 0.62 us: per_device(): grads[512:1024]]
    pallas_call x0 -> x1, Pallas kernels: none -> 1.52 us  [split(): pl.pallas_call(split_kernel, out_shape=tuple((jax.ShapeDtypeStruct((kw, n...]
    unnamed x8 -> x6, local copies, waits for them, and re-layouts: 3.7 us -> 2.48 us
where the time goes in v2:
time: 60.2 us; the launch traced here: 60 us
  Pallas kernels  56 us (93%)
  local copies, waits for them, and re-layouts  3.32 us (6%)
  between operations  0.67 us (1%)
    pallas_call x1, Pallas kernels, reduce(): pl.pallas_call(functools.partial(reduce_kernel, nr, nc), out_shape=jax.Sh...  24.8 us
    pallas_call x1, Pallas kernels, gather(): pl.pallas_call(functools.partial(gather_kernel, nr, nc), out_shape=(shape...  24.6 us
    pallas_call x1, Pallas kernels, block(): pl.pallas_call(block_kernel, out_shape=(shape((8, 16, 512), BF), shape((1...  5.09 us
    unnamed x6, local copies, waits for them, and re-layouts  2.48 us
    pallas_call x1, Pallas kernels, split(): pl.pallas_call(split_kernel, out_shape=tuple((jax.ShapeDtypeStruct((kw, n...  1.52 us

profile of v2, /device:TPU:1, one launch (start us, length us, event | category | flops | bytes accessed | tf_op | source)
XLA Modules:
  0.0 60.0 jit_solution(17785204552510792535)
XLA Ops:
  0.6 0.8 %concatenate.3 = bf16[1280,16]{0,1:T(8,128)(2,1)S(1)} concatenate(bf16[256,16]{0,1:T(8,128)(2,1)} %param.7, bf16[256,16]{0,1:T(8,128)(2,1)} %param.10, bf16[512,16]{0,1:T(8,128)(2,1)} %param.9, bf16[144,16]{0,1:T(8,128)(2,1)} %param.8, bf16[112,16]{0,1:T(8,128)(2,1)S(1)} %broadcast_in_dim.3), dimensions={0} | concatenate | bytes 81920 | tf_op jit(solution)/shard_map/concatenate | solution.py:614
  1.5 0.0 copy-start.1
  1.5 0.9 %copy-done.1 = bf16[16,32,256]{2,1,0:T(8,128)(2,1)S(1)} copy-done((bf16[16,32,256]{2,1,0:T(8,128)(2,1)S(1)}, bf16[16,32,256]{2,1,0:T(8,128)(2,1)}, u32[]{:S(2)}) %copy-start.1) | copy-done | bytes 262168
  2.4 0.0 copy-start.2
  2.4 0.9 %copy-done.2 = bf16[8,16,512]{2,1,0:T(8,128)(2,1)S(1)} copy-done((bf16[8,16,512]{2,1,0:T(8,128)(2,1)S(1)}, bf16[8,16,512]{2,1,0:T(8,128)(2,1)}, u32[]{:S(2)}) %copy-start.2) | copy-done | bytes 131096
  3.3 24.6 %gather.1 = (bf16[8,4,16,1280]{3,2,1,0:T(8,128)(2,1)S(1)}, f32[4,240,256]{2,1,0:T(8,128)S(1)}, f32[4,224,128]{2,1,0:T(8,128)S(1)}) custom-call(bf16[16,1280]{1,0:T(8,128)(2,1)S(1)} %bitcast.9, bf16[16,32,256]{2,1,0:T(8,128)(2,1)S(1)} %copy-done.1, bf16[8,16,512]{2,1,0:T(8,128)(2,1)S(1)} %copy-done.2), custom_call_target="tpu_custom_call" | custom-call | tf_op jit(solution)/shard_map/gather/pallas_call | solution.py:260
  27.9 5.1 %block.1 = (bf16[8,16,512]{2,1,0:T(8,128)(2,1)}, bf16[16,32,256]{2,1,0:T(8,128)(2,1)}, bf16[512,1280]{1,0:T(8,128)(2,1)S(1)}) custom-call(bf16[512,1280]{1,0:T(8,128)(2,1)S(1)} %bitcast.7, f32[4,240,256]{2,1,0:T(8,128)S(1)} %get-tuple-element.17.xp, f32[4,224,128]{2,1,0:T(8,128)S(1)} %get-tuple-element.18.c32), custom_call_target="tpu_custom_call" | custom-call | tf_op jit(solution)/shard_map/block/pallas_call | solution.py:430
  33.0 24.8 %reduce.1.slab = f32[16,1280]{1,0:T(8,128)S(1)} custom-call(bf16[8,4,16,1280]{3,2,1,0:T(8,128)(2,1)S(1)} %bitcast.8), custom_call_target="tpu_custom_call" | custom-call | tf_op jit(solution)/shard_map/reduce/pallas_call | solution.py:569
  57.8 0.0 copy-start
  57.8 0.6 %copy-done = f32[16,1280]{1,0:T(8,128)} copy-done((f32[16,1280]{1,0:T(8,128)}, f32[16,1280]{1,0:T(8,128)S(1)}, u32[]{:S(2)}) %copy-start) | copy-done | bytes 81944
  58.5 1.5 %split.1 = (f32[16,256]{1,0:T(8,128)}, f32[16,144]{1,0:T(8,128)}, f32[16,512]{1,0:T(8,128)}, f32[16,256]{1,0:T(8,128)}) custom-call(f32[16,1280]{1,0:T(8,128)} %copy-done), custom_call_target="tpu_custom_call" | custom-call | tf_op jit(solution)/shard_map/split/pallas_call | solution.py:599
  (1 shorter events, 0.0 us)
Async XLA Ops:
  1.5 1.0 %copy-start.1 = (bf16[16,32,256]{2,1,0:T(8,128)(2,1)S(1)}, bf16[16,32,256]{2,1,0:T(8,128)(2,1)}, u32[]{:S(2)}) copy-start(bf16[16,32,256]{2,1,0:T(8,128)(2,1)} %region.1) | copy-start | bytes 786436
  2.4 0.9 %copy-start.2 = (bf16[8,16,512]{2,1,0:T(8,128)(2,1)S(1)}, bf16[8,16,512]{2,1,0:T(8,128)(2,1)}, u32[]{:S(2)}) copy-start(bf16[8,16,512]{2,1,0:T(8,128)(2,1)} %cot.1) | copy-start | bytes 393220
  57.8 0.6 %copy-start = (f32[16,1280]{1,0:T(8,128)}, f32[16,1280]{1,0:T(8,128)S(1)}, u32[]{:S(2)}) copy-start(f32[16,1280]{1,0:T(8,128)S(1)} %reduce.1.slab) | copy-start | bytes 245764

commit v3 on v2

--- a/solution.py
+++ b/solution.py
@@ -45,8 +45,8 @@
 
 
 def gather_kernel(
-    nr, nc, wt, region, cot, full, xp, c32,
-    regv, cotv, image, lstrip, fstrip, top, bot, cbot, lft, rgt,
+    nr, nc, w_reduce, w_group, w_expand, w_short, region, cot, full, xp, c32,
+    wt, wg, regv, cotv, image, lstrip, fstrip, top, bot, cbot, lft, rgt,
     ls, zs, zr, us, ur, ds, dr_, fs, fr, cs, cr, hs, hr,
 ):
     nz = nc // NY
@@ -88,10 +88,14 @@
     loads = [
         pltpu.make_async_copy(region, regv, ls.at[0]),
         pltpu.make_async_copy(cot, cotv, ls.at[1]),
+        pltpu.make_async_copy(w_reduce, wt.at[:, 0:256], ls.at[2]),
+        pltpu.make_async_copy(w_short, wt.at[:, 256:512], ls.at[3]),
+        pltpu.make_async_copy(w_expand, wt.at[:, 512:1024], ls.at[4]),
+        pltpu.make_async_copy(w_group, wg, ls.at[5]),
     ]
     for load in loads:
         load.start()
-    full[z, y, :, lanes] = wt[:, lanes]
+    wt[:, 1024:] = jnp.zeros_like(wt[:, 1024:])
     image[...] = jnp.zeros_like(image)
     c32[...] = jnp.zeros_like(c32)
 
@@ -121,6 +125,8 @@
 
     for load in loads:
         load.wait()
+    wt[:, 1024:1168] = wg[...]
+    full[z, y, :, lanes] = wt[:, lanes]
     for h in range(2):
         side = slice(128 * h, 128 * h + 128)
         for r in range(16):
@@ -251,9 +257,9 @@
         copy.wait()
 
 
-def gather(nr, nc, wt, region, cot):
+def gather(nr, nc, *arrays):
     nz = nc // NY
-    kw = wt.shape[0]
+    kw = arrays[0].shape[0]
     shape = jax.ShapeDtypeStruct
     hbm = pl.BlockSpec(memory_space=pltpu.HBM)
     dma = pltpu.SemaphoreType.DMA
@@ -264,9 +270,11 @@
             shape((4, 10 * S, 256), F32),
             shape((4, MO, 128), F32),
         ),
-        in_specs=[VMEM, hbm, hbm],
+        in_specs=[hbm] * 6,
         out_specs=(VMEM,) * 3,
         scratch_shapes=[
+            pltpu.VMEM((kw, LANES), BF),
+            pltpu.VMEM((kw, 144), BF),
             pltpu.VMEM((16, 32, 256), BF),
             pltpu.VMEM((8, 16, 512), BF),
             pltpu.VMEM((2, 20 * PW, 128), F32),
@@ -277,7 +285,7 @@
             pltpu.VMEM((16, 512), BF),
             pltpu.VMEM((3, 16, 256), BF),
             pltpu.VMEM((3, 2, 16, 512), BF),
-            dma((2,)),
+            dma((6,)),
             dma((nz,)), dma((nz,)),
             dma((nz,)), dma((nz,)),
             dma((nz,)), dma((nz,)),
@@ -289,7 +297,7 @@
             collective_id=0, has_side_effects=True, vmem_limit_bytes=24 << 20
         ),
         name="gather",
-    )(wt, region, cot)
+    )(*(pltpu.with_memory_space_constraint(a, pltpu.HBM) for a in arrays))
 
 
 def tap_source(tap):
@@ -299,8 +307,8 @@
 
 
 def block_kernel(
-    full, xp, c32, block_out, region_grad, gt,
-    hid, sl1, bdt, h2, sl2, gs, gso, g2, gsot, g2ot, g1, g1t, rg,
+    full, xp, c32, block_out, region_grad, hid, h2, gsot, g2ot, g1t,
+    sl1, bdt, sl2, gs, gso, g2, g1, rg,
 ):
     for k in range(4):
         hid[k, 10 * S :] = jnp.zeros((PLANE - 10 * S, 512), F32)
@@ -363,30 +371,6 @@
         grad = mm(gs[...], full[:, 512 + 256 * t : 768 + 256 * t], NN) * sl2[:, half]
         g2[:, half] = grad.astype(BF).astype(F32)
         g2ot[half, :] = jnp.transpose(jnp.where(own, grad[:MW], 0.0)).astype(BF)
-
-    for n in range(2):
-        half = slice(256 * n, 256 * n + 256)
-        gt[half, 256:512] = mm(gsot[half, :], strided[:MW], NN).astype(BF)
-        for m in range(2):
-            gt[half, 512 + 256 * m : 768 + 256 * m] = mm(
-                gsot[half, :], h2[:MW, 256 * m : 256 * m + 256], NN
-            ).astype(BF)
-    for u in range(4):
-        block = slice(128 * u, 128 * u + 128)
-        sums = [[jnp.zeros((16, 128), F32)] * 8, [jnp.zeros((16, 128), F32)] * 8]
-        for tap in range(9):
-            k, off = tap_source(tap)
-            outer = mm(g2ot[block, :], hid[k, off : off + MW, block].astype(BF), NN)
-            for g in range(8):
-                piece = outer[g * 16 : g * 16 + 16]
-                turn = ((tap % 8 - g) * 16) % 128
-                if turn:
-                    piece = pltpu.roll(piece, turn, 1)
-                sums[tap // 8][g] = jnp.where(lane == tap % 8, piece, sums[tap // 8][g])
-        for h in range(2):
-            for g in range(8):
-                low = u * 128 + g * 16
-                gt[low : low + 16, 1024 + 128 * h : 1152 + 128 * h] = sums[h][g].astype(BF)
 
     for k in range(4):
         pr, pc = divmod(k, 2)
@@ -412,14 +396,6 @@
                 rg[h, pl.ds(line, 16, stride=2), :] = back[
                     i * S : i * S + 16, 128 * h : 128 * h + 128
                 ]
-    for n in range(2):
-        half = slice(256 * n, 256 * n + 256)
-        grad = jnp.zeros((256, 256), F32)
-        for k in range(4):
-            pr, pc = divmod(k, 2)
-            window = (1 - pr) * S + (1 - pc)
-            grad = grad + mm(g1t[k, half, :], xp[k, window : window + MW].astype(BF), NN)
-        gt[half, 0:256] = grad.astype(BF)
     for r in range(16):
         for h in range(2):
             region_grad[r, :, 128 * h : 128 * h + 128] = rg[h, 32 * r : 32 * r + 32].astype(BF)
@@ -432,23 +408,22 @@
         out_shape=(
             shape((8, 16, 512), BF),
             shape((16, 32, 256), BF),
-            shape((512, LANES), BF),
+            shape((4, PLANE, 512), F32),
+            shape((MO, 512), BF),
+            shape((512, MW), BF),
+            shape((512, MW), BF),
+            shape((4, 512, MW), BF),
         ),
         in_specs=[VMEM] * 3,
-        out_specs=(VMEM,) * 3,
+        out_specs=(VMEM,) * 7,
         scratch_shapes=[
             pltpu.VMEM((4, PLANE, 512), F32),
-            pltpu.VMEM((4, PLANE, 512), F32),
             pltpu.VMEM((9, 2, 256, 256), BF),
-            pltpu.VMEM((MO, 512), BF),
             pltpu.VMEM((MO, 512), F32),
             pltpu.VMEM((MO, 512), BF),
             pltpu.VMEM((MW, 512), BF),
             pltpu.VMEM((MO, 512), F32),
-            pltpu.VMEM((512, MW), BF),
-            pltpu.VMEM((512, MW), BF),
             pltpu.VMEM((4, MW, 512), BF),
-            pltpu.VMEM((4, 512, MW), BF),
             pltpu.VMEM((2, 512, 128), F32),
         ],
         compiler_params=pltpu.CompilerParams(vmem_limit_bytes=40 << 20),
@@ -456,8 +431,45 @@
     )(full, xp, c32)
 
 
+def weight_grads(xp, hid, h2, gsot, g2ot, g1t, gt):
+    def put(first, lanes, value):
+        blocks = value.reshape(value.shape[0] // (NY * GW), NY, GW, value.shape[1])
+        gt[pl.ds(first // (NY * GW), blocks.shape[0]), :, :, lanes] = blocks.astype(BF)
+
+    strided = xp[3, :MW].astype(BF)
+    for n in range(2):
+        half = slice(256 * n, 256 * n + 256)
+        put(256 * n, slice(256, 512), mm(gsot[half, :], strided, NN))
+        for m in range(2):
+            cols = slice(256 * m, 256 * m + 256)
+            put(256 * n, slice(512 + 256 * m, 768 + 256 * m), mm(gsot[half, :], h2[:MW, cols], NN))
+        grad = jnp.zeros((256, 256), F32)
+        for k in range(4):
+            pr, pc = divmod(k, 2)
+            window = (1 - pr) * S + (1 - pc)
+            grad = grad + mm(g1t[k, half, :], xp[k, window : window + MW].astype(BF), NN)
+        put(256 * n, slice(0, 256), grad)
+    lane = lax.broadcasted_iota(jnp.int32, (16, 128), 1) // GW
+    for u in range(4):
+        block = slice(128 * u, 128 * u + 128)
+        sums = [[jnp.zeros((16, 128), F32)] * 8, [jnp.zeros((16, 128), F32)] * 8]
+        for tap in range(9):
+            k, off = tap_source(tap)
+            outer = mm(g2ot[block, :], hid[k, off : off + MW, block].astype(BF), NN)
+            for g in range(8):
+                piece = outer[g * 16 : g * 16 + 16]
+                turn = ((tap % 8 - g) * 16) % 128
+                if turn:
+                    piece = pltpu.roll(piece, turn, 1)
+                sums[tap // 8][g] = jnp.where(lane == tap % 8, piece, sums[tap // 8][g])
+        for h in range(2):
+            for g in range(8):
+                at = divmod(8 * u + g, NY)
+                gt[at[0], at[1], :, 1024 + 128 * h : 1152 + 128 * h] = sums[h][g].astype(BF)
+
+
 def reduce_kernel(
-    nr, nc, gt, out, rc, send, land, s2, rz, rx,
+    nr, nc, xp, hid, h2, gsot, g2ot, g1t, out, gt, rc, send, land, s2, rz, rx,
     cs, cr, ys, yr, zs, zr, xs, xr, fs, fr,
 ):
     nz, nx = nc // NY, nr // 2
@@ -482,6 +494,7 @@
         greet(row, lax.rem(z + d, nz) * NY + y)
     for d in range(1, nx):
         greet(2 * lax.rem(x + d, nx) + core, col)
+    weight_grads(xp, hid, h2, gsot, g2ot, g1t, gt)
     pl.semaphore_wait(barrier, 3 + nz - 1 + nx - 1)
 
     across = []
@@ -562,16 +575,17 @@
     final.wait()
 
 
-def reduce(nr, nc, gt):
+def reduce(nr, nc, *arrays):
     nz, nx = nc // NY, nr // 2
-    kw = gt.shape[2]
+    kw = GW
     dma = pltpu.SemaphoreType.DMA
     return pl.pallas_call(
         functools.partial(reduce_kernel, nr, nc),
         out_shape=jax.ShapeDtypeStruct((kw, LANES), F32),
-        in_specs=[VMEM],
+        in_specs=[VMEM] * 6,
         out_specs=VMEM,
         scratch_shapes=[
+            pltpu.VMEM((nz, NY, kw, LANES), BF),
             pltpu.VMEM((nz, NY, kw, HALF), BF),
             pltpu.VMEM((6, nz // 2, kw, HALF), BF),
             pltpu.VMEM((6, nz // 2, kw, HALF), BF),
@@ -584,14 +598,22 @@
             collective_id=1, has_side_effects=True, vmem_limit_bytes=24 << 20
         ),
         name="reduce",
-    )(gt)
-
-
-def split_kernel(slab, reduce_grad, group_grad, expand_grad, shortcut_grad):
-    reduce_grad[...] = slab[:, 0:256]
-    shortcut_grad[...] = slab[:, 256:512]
-    expand_grad[...] = slab[:, 512:1024]
-    group_grad[...] = slab[:, 1024:1168]
+    )(*arrays)
+
+
+def split_kernel(slab, reduce_grad, group_grad, expand_grad, shortcut_grad, group, sems):
+    copies = [
+        pltpu.make_async_copy(slab.at[:, 0:256], reduce_grad, sems.at[0]),
+        pltpu.make_async_copy(slab.at[:, 256:512], shortcut_grad, sems.at[1]),
+        pltpu.make_async_copy(slab.at[:, 512:1024], expand_grad, sems.at[2]),
+        pltpu.make_async_copy(group, group_grad, sems.at[3]),
+    ]
+    for copy in copies[:3]:
+        copy.start()
+    group[...] = slab[:, 1024:1168]
+    copies[3].start()
+    for copy in copies:
+        copy.wait()
 
 
 def split(slab):
@@ -600,7 +622,9 @@
         split_kernel,
         out_shape=tuple(jax.ShapeDtypeStruct((kw, n), F32) for n in (256, 144, 512, 256)),
         in_specs=[VMEM],
-        out_specs=(VMEM,) * 4,
+        out_specs=(pl.BlockSpec(memory_space=pltpu.HBM),) * 4,
+        scratch_shapes=[pltpu.VMEM((kw, 144), F32), pltpu.SemaphoreType.DMA((4,))],
+        compiler_params=pltpu.CompilerParams(vmem_limit_bytes=2 << 20),
         name="split",
     )(slab)
 
@@ -609,14 +633,12 @@
     nr, nc = mesh.shape["row"], mesh.shape["col"]
 
     def per_device(region, reduce_weight, group_weight, expand_weight, shortcut_weight, cotangent):
-        kw = reduce_weight.shape[1]
-        blank = jnp.zeros((LANES - 1168, kw), BF)
-        wt = jnp.concatenate(
-            [reduce_weight, shortcut_weight, expand_weight, group_weight, blank], axis=0
-        ).T
-        full, xp, c32 = gather(nr, nc, wt, region, cotangent)
-        block_out, region_grad, gt = block(full.reshape(512, LANES), xp, c32)
-        grads = split(reduce(nr, nc, gt.reshape(nc // NY, NY, kw, LANES)))
+        full, xp, c32 = gather(
+            nr, nc, reduce_weight.T, group_weight.T, expand_weight.T, shortcut_weight.T,
+            region, cotangent,
+        )
+        block_out, region_grad, *terms = block(full.reshape(512, LANES), xp, c32)
+        grads = split(reduce(nr, nc, xp, *terms))
         return (block_out, region_grad, *(grad.T for grad in grads))
 
     weight = P(None, "col")

time: 60.2 us -> 55.1 us (0.915)
  local copies, waits for them, and re-layouts: 3.32 us -> 0 us
  Pallas kernels: 56 us -> 54.3 us
    unnamed x6 -> x0, local copies, waits for them, and re-layouts: 2.48 us -> none
    pallas_call x1, Pallas kernels: 5.09 us -> 4.17 us  [block(): pl.pallas_call(block_kernel, out_shape=(shape((8, 16, 512), BF), shape((1...]
    pallas_call x1, Pallas kernels: 1.52 us -> 0.67 us  [split(): pl.pallas_call(split_kernel, out_shape=tuple((jax.ShapeDtypeStruct((kw, n...]
    concatenate x1 -> x0, local copies, waits for them, and re-layouts: 0.84 us -> none  [per_device(): jnp.concatenate([reduce_weight, shortcut_weight, expand_weight, group_wei...]
    pallas_call x1, Pallas kernels: 24.8 us -> 25.5 us  [reduce(): pl.pallas_call(functools.partial(reduce_kernel, nr, nc), out_shape=jax.Sh...]
where the time goes in v3:
time: 55.1 us; the launch traced here: 55 us
  Pallas kernels  54.3 us (99%)
  between operations  0.65 us (1%)
    pallas_call x1, Pallas kernels, reduce(): pl.pallas_call(functools.partial(reduce_kernel, nr, nc), out_shape=jax.Sh...  25.5 us
    pallas_call x1, Pallas kernels, gather(): pl.pallas_call(functools.partial(gather_kernel, nr, nc), out_shape=(shape...  24 us
    pallas_call x1, Pallas kernels, block(): pl.pallas_call(block_kernel, out_shape=(shape((8, 16, 512), BF), shape((1...  4.17 us

profile of v3, /device:TPU:1, one launch (start us, length us, event | category | flops | bytes accessed | tf_op | source)
XLA Modules:
  0.0 55.0 jit_solution(15340998690684779504)
XLA Ops:
  0.6 24.0 %gather.1 = (bf16[8,4,16,1280]{3,2,1,0:T(8,128)(2,1)S(1)}, f32[4,240,256]{2,1,0:T(8,128)S(1)}, f32[4,224,128]{2,1,0:T(8,128)S(1)}) custom-call(bf16[16,256]{1,0:T(8,128)(2,1)} %bitcast.11, bf16[16,144]{1,0:T(8,128)(2,1)} %bitcast.12, bf16[16,512]{1,0:T(8,128)(2,1)} %bitcast.10, bf16[16,256]{1,0:T(8,128)(2,1)} %bitcast.13, bf16[16,32,256]{2,1,0:T(8,128)(2,1)} %region.1, ...), custom_call_target="tpu_custom_call" | custom-call | tf_op jit(solution)/shard_map/gather/pallas_call | solution.py:266
  24.6 4.2 %block.1 = (bf16[8,16,512]{2,1,0:T(8,128)(2,1)}, bf16[16,32,256]{2,1,0:T(8,128)(2,1)}, f32[4,256,512]{2,1,0:T(8,128)S(1)}, bf16[224,512]{1,0:T(8,128)(2,1)S(1)},...) custom-call(bf16[512,1280]{1,0:T(8,128)(2,1)S(1)} %bitcast.9, ...), custom_call_target="tpu_custom_call" | custom-call | tf_op jit(solution)/shard_map/block/pallas_call | solution.py:406
  28.8 25.5 %reduce.1.slab = f32[16,1280]{1,0:T(8,128)S(1)} custom-call(f32[4,240,256]{2,1,0:T(8,128)S(1)} %get-tuple-element.21.xp, f32[4,256,512]{2,1,0:T(8,128)S(1)} %get-tuple-element.25.hid, bf16[224,512]{1,0:T(8,128)(2,1)S(1)} %get-tuple-element.26.h2, bf16[512,192]{1,0:T(8,128)(2,1)S(1)} %get-tuple-element.27.gsot, bf16[512,192]{1,0:T(8,128)(2,1)S(1)} %get-tuple-element.28.g2ot, ...), custom_call_target="tpu_custom_call" | custom-call | tf_op jit(solution)/shard_map/reduce/pallas_call | solution.py:582
  54.3 0.7 %split.1 = (f32[16,256]{1,0:T(8,128)}, f32[16,144]{1,0:T(8,128)}, f32[16,512]{1,0:T(8,128)}, f32[16,256]{1,0:T(8,128)}) custom-call(f32[16,1280]{1,0:T(8,128)S(1)} %reduce.1.slab), custom_call_target="tpu_custom_call" | custom-call | tf_op jit(solution)/shard_map/split/pallas_call | solution.py:621

commit v4 on v2

v4 whole, which is shorter than its diff:
```python
import functools

import jax
import jax.numpy as jnp
from jax import lax
from jax.experimental import pallas as pl
from jax.experimental.pallas import tpu as pltpu
from jax.sharding import PartitionSpec as P

MESH = pl.DeviceIdType.MESH
BF = jnp.bfloat16
F32 = jnp.float32
NY = 4
GW = 16
LANES = 1280
HALF = LANES // 2
CHUNKS = ((0, 256), (512, 384))
LOCAL = (slice(0, 256), slice(256, 640))
S = 24
PLANE = 256
MO = 224
MW = 192
PW = 48
VMEM = pl.BlockSpec(memory_space=pltpu.VMEM)

NN = (((1,), (0,)), ((), ()))
NT = (((1,), (1,)), ((), ()))


def mm(lhs, rhs, dims):
    return lax.dot_general(lhs, rhs, dims, preferred_element_type=F32)


def sigmoid(value):
    return 0.5 * jnp.tanh(0.5 * value) + 0.5


def remote(src, dst, send_sem, recv_sem, row, col):
    return pltpu.make_async_remote_copy(
        src_ref=src,
        dst_ref=dst,
        send_sem=send_sem,
        recv_sem=recv_sem,
        device_id=(row, col),
        device_id_type=MESH,
    )


def tap_source(tap):
    a, b = divmod(tap, 3)
    plane = (a % 2) * 2 + b % 2
    return plane, (a == 2) * S + (b == 2)


def front(full, xp, hid, sl1, bdt, h2, sl2):
    weight = full[:, :, :, 0:256].reshape(512, 256)
    for k in range(4):
        hid[k, 10 * S :] = jnp.zeros((PLANE - 10 * S, 512), F32)
        pixels = xp[k].astype(BF)
        for n in range(2):
            half = slice(256 * n, 256 * n + 256)
            pre = mm(pixels, weight[half], NT)
            gate = sigmoid(pre)
            act = pre * gate
            hid[k, : 10 * S, half] = act.astype(BF).astype(F32)
            sl1[k, : 10 * S, half] = gate + act * (1.0 - gate)

    lane = lax.broadcasted_iota(jnp.int32, (16, 128), 1) // GW
    for tap in range(9):
        first = 256 + 128 * (tap // 8)
        for u in range(4):
            t, v = divmod(u, 2)
            for g in range(8):
                at = divmod(8 * u + g, NY)
                piece = full[at[0], at[1], :, first : first + 128].astype(F32)
                turn = ((g - tap % 8) * 16) % 128
                if turn:
                    piece = pltpu.roll(piece, turn, 1)
                piece = jnp.where(lane == g, piece, 0.0).astype(BF)
                low = v * 128 + g * 16
                bdt[tap, t, low : low + 16, v * 128 : v * 128 + 128] = piece
                bdt[tap, t, low : low + 16, (1 - v) * 128 : (1 - v) * 128 + 128] = jnp.zeros(
                    (16, 128), BF
                )

    for t in range(2):
        half = slice(256 * t, 256 * t + 256)
        pre = jnp.zeros((MO, 256), F32)
        for tap in range(9):
            k, off = tap_source(tap)
            pre = pre + mm(hid[k, off : off + MO, half].astype(BF), bdt[tap, t], NT)
        gate = sigmoid(pre)
        act = pre * gate
        h2[:, half] = act.astype(BF)
        sl2[:, half] = gate + act * (1.0 - gate)


def whole_kernel(
    nr, nc, w_reduce, w_group, w_expand, w_short, region, cot,
    block_out, region_grad, out,
    full, xp, c32, hid, sl1, bdt, h2, sl2, wt, wg, regv, cotv, image, lstrip, fstrip, top, bot, cbot, lft, rgt,
    gsot, g2ot, g1t, gs, gso, g2, g1, rg, gt, rc, send, land, s2, rz, rx,
    ls, zs, zr, us, ur, ds, dr_, fs, fr, cs, cr, hs, hr,
    rcs, rcr, rys, ryr, rzs, rzr, rxs, rxr, rfs, rfr,
):
    nz, nx, nh = nc // NY, nr // 2, nc // NY // 2
    row, col = lax.axis_index("row"), lax.axis_index("col")
    x, core = row // 2, lax.rem(row, 2)
    partner = row + 1 - 2 * core
    z, y = col // NY, lax.rem(col, NY)
    y_up, y_down, y_far = lax.rem(y + 1, NY), lax.rem(y + NY - 1, NY), lax.rem(y + 2, NY)
    lanes = pl.ds(pl.multiple_of(core * HALF, 128), HALF)
    has_up, has_down = row > 0, row < nr - 1
    has_left, has_right = col > 0, col < nc - 1

    barrier = pltpu.get_barrier_semaphore()

    def greet(to_row, to_col):
        pl.semaphore_signal(barrier, inc=1, device_id=(to_row, to_col), device_id_type=MESH)

    for d in range(1, nz):
        greet(row, lax.rem(z + d, nz) * NY + y)
    greet(row, z * NY + y_up)
    greet(row, z * NY + y_down)
    greet(partner, col)
    for d in range(1, nx):
        greet(2 * lax.rem(x + d, nx) + core, col)
    count = nz + 2 + nx - 1
    for dr in (-1, 0, 1):
        for dc in (-1, 0, 1):
            if dr == 0 and dc == 0:
                continue
            there = None
            for step, less, more in ((dr, has_up, has_down), (dc, has_left, has_right)):
                if step:
                    flag = more if step > 0 else less
                    there = flag if there is None else there & flag
            count = count + there.astype(jnp.int32)

            @pl.when(there)
            def _(dr=dr, dc=dc):
                greet(row + dr, col + dc)

    loads = [
        pltpu.make_async_copy(region, regv, ls.at[0]),
        pltpu.make_async_copy(cot, cotv, ls.at[1]),
        pltpu.make_async_copy(w_reduce, wt.at[:, 0:256], ls.at[2]),
        pltpu.make_async_copy(w_short, wt.at[:, 512:768], ls.at[3]),
        pltpu.make_async_copy(w_expand, wt.at[:, 768:1280], ls.at[4]),
        pltpu.make_async_copy(w_group, wg, ls.at[5]),
    ]
    for load in loads:
        load.start()
    wt[:, 256:512] = jnp.zeros((wt.shape[0], 256), BF)
    image[...] = jnp.zeros_like(image)
    c32[...] = jnp.zeros_like(c32)

    plan = [
        (has_down, 1, 0, regv.at[15], top, 0),
        (has_up, -1, 0, regv.at[pl.ds(0, 2)], bot, 1),
        (has_up, -1, 0, cotv.at[0], cbot, 2),
    ]
    for k, (there, step) in enumerate(((has_down, 1), (None, 0), (has_up, -1))):
        right = has_right if there is None else has_right & there
        left = has_left if there is None else has_left & there
        plan.append((right, step, 1, lstrip, lft.at[k], 3 + k))
        plan.append((left, step, -1, fstrip, rgt.at[k], 6 + k))
    above = {0: has_up, 1: has_down, 2: has_down}
    for k, there in enumerate((has_up, None, has_down)):
        above[3 + k] = has_left if there is None else has_left & there
        above[6 + k] = has_right if there is None else has_right & there
    zero_of = {0: top, 1: bot, 2: cbot}
    for k in range(3):
        zero_of[3 + k] = lft.at[k]
        zero_of[6 + k] = rgt.at[k]
    for n, ref in zero_of.items():

        @pl.when(jnp.logical_not(above[n]))
        def _(ref=ref):
            ref[...] = jnp.zeros(ref.shape, ref.dtype)

    for load in loads:
        load.wait()
    wt[:, 256:400] = wg[...]
    full[z, y, :, lanes] = wt[:, lanes]
    for h in range(2):
        side = slice(128 * h, 128 * h + 128)
        for r in range(16):
            image[h, (r + 1) * PW + 1 : (r + 1) * PW + 33] = regv[r, :, side].astype(F32)
        lstrip[:, side] = image[h, pl.ds(PW + 32, 16, stride=PW), :].astype(BF)
        for q in range(2):
            fstrip[0, :, 256 * q + 128 * h : 256 * q + 128 * h + 128] = image[
                h, pl.ds(PW + 1 + q, 16, stride=PW), :
            ].astype(BF)
    for h in range(4):
        side = slice(128 * h, 128 * h + 128)
        for i in range(8):
            c32[h, i * S : i * S + 16] = cotv[i, :, side].astype(F32)
        first = c32[h, pl.ds(0, 8, stride=S), :]
        fstrip[1, :, side] = jnp.concatenate([first, jnp.zeros_like(first)], axis=0).astype(BF)

    pl.semaphore_wait(barrier, count)

    order = [nz // 2] + [n for d in range(nz // 2 - 1, 0, -1) for n in (d, nz - d)]
    along_z, upward, downward, forward = {}, {}, {}, {}
    for d in order:
        copy = remote(
            wt.at[:, lanes], full.at[z, y, :, lanes], zs.at[d], zr.at[d],
            row, lax.rem(z + d, nz) * NY + y,
        )
        copy.start()
        along_z[d] = copy

    def to_neighbours(d):
        here = full.at[lax.rem(z + nz - d, nz), y, :, lanes]
        upward[d] = remote(here, here, us.at[d], ur.at[d], row, z * NY + y_up)
        downward[d] = remote(here, here, ds.at[d], dr_.at[d], row, z * NY + y_down)
        upward[d].start()
        downward[d].start()

    to_neighbours(0)
    halos = []
    for there, dr, dc, src, dst, n in plan:
        copy = remote(src, dst, hs.at[n], hr.at[n], row + dr, col + dc)
        halos.append((there, copy, n))

        @pl.when(there)
        def _(copy=copy):
            copy.start()

    nearest = [0] + order[::-1]
    for d in nearest[1:]:
        along_z[d].wait_recv()
        to_neighbours(d)

    columns = []

    def column(at):
        block = full.at[:, at, :, lanes]
        n = len(columns)
        copy = remote(block, block, cs.at[n], cr.at[n], partner, col)
        copy.start()
        columns.append(copy)

    column(y)

    for d in nearest:
        b = lax.rem(z + nz - d, nz)
        upward[d].wait_recv()
        if d % 2 == 0:
            here = full.at[b, y_down, :, lanes]
            forward[d] = remote(here, here, fs.at[d], fr.at[d], row, z * NY + y_up)
            forward[d].start()
        downward[d].wait_recv()
        if d % 2 == 1:
            here = full.at[b, y_up, :, lanes]
            forward[d] = remote(here, here, fs.at[d], fr.at[d], row, z * NY + y_down)
            forward[d].start()
    column(y_up)
    column(y_down)

    for there, copy, n in halos:

        @pl.when(above[n])
        def _(copy=copy):
            copy.wait_recv()

    for h in range(2):
        side = slice(128 * h, 128 * h + 128)
        image[h, 1:33] = top[:, side].astype(F32)
        for r in range(2):
            image[h, (17 + r) * PW + 1 : (17 + r) * PW + 33] = bot[r, :, side].astype(F32)
        image[h, pl.ds(PW, 16, stride=PW), :] = lft[1, :, side].astype(F32)
        image[h, 0:1] = lft[0, :, side].astype(F32)[15:16]
        below = lft[2, :, side].astype(F32)
        for r in range(2):
            image[h, (17 + r) * PW : (17 + r) * PW + 1] = below[r : r + 1]
        for q in range(2):
            side = slice(256 * q + 128 * h, 256 * q + 128 * h + 128)
            image[h, pl.ds(PW + 33 + q, 16, stride=PW), :] = rgt[1, 0, :, side].astype(F32)
            image[h, 33 + q : 34 + q] = rgt[0, 0, :, side].astype(F32)[15:16]
            corner = rgt[2, 0, :, side].astype(F32)
            for r in range(2):
                low = (17 + r) * PW + 33 + q
                image[h, low : low + 1] = corner[r : r + 1]
    for h in range(4):
        side = slice(128 * h, 128 * h + 128)
        c32[h, 8 * S : 8 * S + 16] = cbot[:, side].astype(F32)
        c32[h, pl.ds(16, 8, stride=S), :] = rgt[1, 1, :, side].astype(F32)[0:8]
        c32[h, 8 * S + 16 : 8 * S + 17] = rgt[2, 1, :, side].astype(F32)[0:1]
    for k in range(4):
        pr, pc = divmod(k, 2)
        for i in range(10):
            for h in range(2):
                xp[k, i * S : (i + 1) * S, 128 * h : 128 * h + 128] = image[
                    h, pl.ds((2 * i + pr) * PW + pc, S, stride=2), :
                ]

    for d in nearest:
        forward[d].wait_recv()
    column(y_far)
    for copy in columns:
        copy.wait_recv()

    front(full, xp, hid, sl1, bdt, h2, sl2)
    w_r = full[:, :, :, 0:256].reshape(512, 256)
    w_s = full[:, :, :, 512:768].reshape(512, 256)
    w_e = full[:, :, :, 768:1280].reshape(512, 512)
    mine = [pl.ds(pl.multiple_of(first + core * wide, 128), wide) for first, wide in CHUNKS]
    other = [pl.ds(pl.multiple_of(first + (1 - core) * wide, 128), wide) for first, wide in CHUNKS]
    chunks = (1, 0)

    across, along_y, turn_z, along_x, final = {}, {}, {}, {}, {}

    def start_across(q):
        for n, at in enumerate((y_far, y_up, y_down, y)):
            copy = remote(
                gt.at[:, at, :, other[q]], rc.at[:, at, :, LOCAL[q]],
                rcs.at[q, n], rcr.at[q, n], partner, col,
            )
            copy.start()
            across[q, n] = copy

    def chip(q, n, at):
        return gt[n, at, :, mine[q]].astype(F32) + rc[n, at, :, LOCAL[q]].astype(F32)

    def start_y(q, n, to):
        copy = remote(
            send.at[n, :, :, LOCAL[q]], land.at[n, :, :, LOCAL[q]],
            rys.at[q, n], ryr.at[q, n], row, z * NY + to,
        )
        copy.start()
        along_y[q, n] = copy

    def fill(q, n, low, at, extra=None):
        for k in range(nh):
            term = chip(q, low + k, at)
            if extra is not None:
                term = term + land[extra, k, :, LOCAL[q]].astype(F32)
            send[n, k, :, LOCAL[q]] = term.astype(BF)

    def y_first(q):
        across[q, 0].wait_recv()
        fill(q, 0, 0, y_far)
        start_y(q, 0, y_up)
        fill(q, 1, nh, y_far)
        start_y(q, 1, y_down)
        across[q, 1].wait_recv()
        fill(q, 2, nh, y_up)
        start_y(q, 2, y_up)
        across[q, 2].wait_recv()
        fill(q, 3, 0, y_down)
        start_y(q, 3, y_down)

    def y_second(q):
        along_y[q, 0].wait_recv()
        fill(q, 4, 0, y_up, 0)
        start_y(q, 4, y_up)
        along_y[q, 1].wait_recv()
        fill(q, 5, nh, y_down, 1)
        start_y(q, 5, y_down)

    def put(first, lanes, value):
        blocks = value.reshape(value.shape[0] // (NY * GW), NY, GW, value.shape[1])
        gt[pl.ds(first // (NY * GW), blocks.shape[0]), :, :, lanes] = blocks.astype(BF)

    own = lax.rem(lax.broadcasted_iota(jnp.int32, (MW, 256), 0), S) < 16
    strided = xp[3, :MO].astype(BF)
    for n in range(2):
        half = slice(256 * n, 256 * n + 256)
        total = mm(h2[...], w_e[half], NT) + mm(strided, w_s[half], NT)
        gate = sigmoid(total)
        act = total * gate
        for i in range(8):
            block_out[i, :, half] = act[i * S : i * S + 16].astype(BF)
        cots = jnp.concatenate([c32[2 * n], c32[2 * n + 1]], axis=1)
        grad = cots * (gate + act * (1.0 - gate))
        gs[:, half] = grad.astype(BF)
        kept = jnp.where(own, grad[:MW], 0.0)
        gso[:, half] = kept.astype(BF)
        gsot[half, :] = jnp.transpose(kept).astype(BF)

    for n in range(2):
        half = slice(256 * n, 256 * n + 256)
        put(256 * n, slice(512, 768), mm(gsot[half, :], strided[:MW], NN))
        for m in range(2):
            cols = slice(256 * m, 256 * m + 256)
            put(256 * n, slice(768 + 256 * m, 1024 + 256 * m), mm(gsot[half, :], h2[:MW, cols], NN))
    start_across(1)

    for t in range(2):
        half = slice(256 * t, 256 * t + 256)
        grad = mm(gs[...], w_e[:, 256 * t : 256 * t + 256], NN) * sl2[:, half]
        g2[:, half] = grad.astype(BF).astype(F32)
        g2ot[half, :] = jnp.transpose(jnp.where(own, grad[:MW], 0.0)).astype(BF)

    lane = lax.broadcasted_iota(jnp.int32, (16, 128), 1) // GW
    for u in range(4):
        block = slice(128 * u, 128 * u + 128)
        sums = [[jnp.zeros((16, 128), F32)] * 8, [jnp.zeros((16, 128), F32)] * 8]
        for tap in range(9):
            k, off = tap_source(tap)
            outer = mm(g2ot[block, :], hid[k, off : off + MW, block].astype(BF), NN)
            for g in range(8):
                piece = outer[g * 16 : g * 16 + 16]
                turn = ((tap % 8 - g) * 16) % 128
                if turn:
                    piece = pltpu.roll(piece, turn, 1)
                sums[tap // 8][g] = jnp.where(lane == tap % 8, piece, sums[tap // 8][g])
        for h in range(2):
            for g in range(8):
                at = divmod(8 * u + g, NY)
                gt[at[0], at[1], :, 256 + 128 * h : 384 + 128 * h] = sums[h][g].astype(BF)


    y_first(1)

    for k in range(4):
        pr, pc = divmod(k, 2)
        window = (1 - pr) * S + (1 - pc)
        for t in range(2):
            half = slice(256 * t, 256 * t + 256)
            spread = jnp.zeros((MW, 256), F32)
            for tap in range(9):
                a, b = divmod(tap, 3)
                if tap_source(tap)[0] != k:
                    continue
                off = (a == 0) * S + (b == 0)
                spread = spread + mm(g2[off : off + MW, half].astype(BF), bdt[tap, t], NN)
            grad = jnp.where(own, spread * sl1[k, window : window + MW, half], 0.0)
            g1[k, :, half] = grad.astype(BF)
            g1t[k, half, :] = jnp.transpose(grad).astype(BF)
    for n in range(2):
        half = slice(256 * n, 256 * n + 256)
        grad = jnp.zeros((256, 256), F32)
        for k in range(4):
            pr, pc = divmod(k, 2)
            window = (1 - pr) * S + (1 - pc)
            grad = grad + mm(g1t[k, half, :], xp[k, window : window + MW].astype(BF), NN)
        put(256 * n, slice(0, 256), grad)
    start_across(0)

    for k in range(4):
        pr, pc = divmod(k, 2)
        back = mm(g1[k], w_r, NN)
        if k == 3:
            back = back + mm(gso[...], w_s, NN)
        for i in range(8):
            line = (2 * i + 1 - pr) * 32 + 1 - pc
            for h in range(2):
                rg[h, pl.ds(line, 16, stride=2), :] = back[
                    i * S : i * S + 16, 128 * h : 128 * h + 128
                ]
    y_first(0)
    y_second(1)
    for r in range(16):
        for h in range(2):
            region_grad[r, :, 128 * h : 128 * h + 128] = rg[h, 32 * r : 32 * r + 32].astype(BF)
    y_second(0)

    for q in chunks:
        part = LOCAL[q]
        across[q, 3].wait_recv()
        for n in (2, 3, 4, 5):
            along_y[q, n].wait_recv()
        for k in range(nh):
            s2[k, :, part] = (
                chip(q, k, y) + land[3, k, :, part].astype(F32) + land[4, k, :, part].astype(F32)
            )
            s2[nh + k, :, part] = (
                chip(q, nh + k, y) + land[2, k, :, part].astype(F32) + land[5, k, :, part].astype(F32)
            )
        for d in order:
            to = lax.rem(z + d, nz)
            rz[0, d, :, part] = s2[to, :, part].astype(BF)
            copy = remote(
                rz.at[0, d, :, part], rz.at[1, d, :, part], rzs.at[q, d], rzr.at[q, d], row, to * NY + y
            )
            copy.start()
            turn_z[q, d] = copy
    for q in chunks:
        part = LOCAL[q]
        term = s2[z, :, part]
        for d in range(1, nz):
            turn_z[q, d].wait_recv()
            term = term + rz[1, d, :, part].astype(F32)
        rx[x, :, part] = term
        for d in range(1, nx):
            here = rx.at[x, :, part]
            copy = remote(
                here, here, rxs.at[q, d], rxr.at[q, d], 2 * lax.rem(x + d, nx) + core, col
            )
            copy.start()
            along_x[q, d] = copy
    for q in chunks:
        part = LOCAL[q]
        for d in range(1, nx):
            along_x[q, d].wait_recv()
        term = rx[0, :, part]
        for n in range(1, nx):
            term = term + rx[n, :, part]
        out[:, mine[q]] = term
        here = out.at[:, mine[q]]
        final[q] = remote(here, here, rfs.at[q], rfr.at[q], partner, col)
        final[q].start()
    for there, copy, n in halos:

        @pl.when(there)
        def _(copy=copy):
            copy.wait_send()

    for copy in columns:
        copy.wait_send()
    for group in (along_z, upward, downward, forward, across, along_y, turn_z, along_x):
        for copy in group.values():
            copy.wait_send()
    for copy in final.values():
        copy.wait()


def whole(nr, nc, *arrays):
    nz, nx = nc // NY, nr // 2
    kw = GW
    shape = jax.ShapeDtypeStruct
    hbm = pl.BlockSpec(memory_space=pltpu.HBM)
    dma = pltpu.SemaphoreType.DMA
    return pl.pallas_call(
        functools.partial(whole_kernel, nr, nc),
        out_shape=(
            shape((8, 16, 512), BF),
            shape((16, 32, 256), BF),
            shape((kw, LANES), F32),
        ),
        in_specs=[hbm] * 6,
        out_specs=(VMEM,) * 3,
        scratch_shapes=[
            pltpu.VMEM((nz, NY, kw, LANES), BF),
            pltpu.VMEM((4, 10 * S, 256), F32),
            pltpu.VMEM((4, MO, 128), F32),
            pltpu.VMEM((4, PLANE, 512), F32),
            pltpu.VMEM((4, PLANE, 512), F32),
            pltpu.VMEM((9, 2, 256, 256), BF),
            pltpu.VMEM((MO, 512), BF),
            pltpu.VMEM((MO, 512), F32),
            pltpu.VMEM((kw, LANES), BF),
            pltpu.VMEM((kw, 144), BF),
            pltpu.VMEM((16, 32, 256), BF),
            pltpu.VMEM((8, 16, 512), BF),
            pltpu.VMEM((2, 20 * PW, 128), F32),
            pltpu.VMEM((16, 256), BF),
            pltpu.VMEM((2, 16, 512), BF),
            pltpu.VMEM((32, 256), BF),
            pltpu.VMEM((2, 32, 256), BF),
            pltpu.VMEM((16, 512), BF),
            pltpu.VMEM((3, 16, 256), BF),
            pltpu.VMEM((3, 2, 16, 512), BF),
            pltpu.VMEM((512, MW), BF),
            pltpu.VMEM((512, MW), BF),
            pltpu.VMEM((4, 512, MW), BF),
            pltpu.VMEM((MO, 512), BF),
            pltpu.VMEM((MW, 512), BF),
            pltpu.VMEM((MO, 512), F32),
            pltpu.VMEM((4, MW, 512), BF),
            pltpu.VMEM((2, 512, 128), F32),
            pltpu.VMEM((nz, NY, kw, LANES), BF),
            pltpu.VMEM((nz, NY, kw, HALF), BF),
            pltpu.VMEM((6, nz // 2, kw, HALF), BF),
            pltpu.VMEM((6, nz // 2, kw, HALF), BF),
            pltpu.VMEM((nz, kw, HALF), F32),
            pltpu.VMEM((2, nz, kw, HALF), BF),
            pltpu.VMEM((nx, kw, HALF), F32),
            dma((6,)),
            dma((nz,)), dma((nz,)), dma((nz,)), dma((nz,)),
            dma((nz,)), dma((nz,)), dma((nz,)), dma((nz,)),
            dma((4,)), dma((4,)), dma((9,)), dma((9,)),
            dma((2, 4)), dma((2, 4)), dma((2, 6)), dma((2, 6)),
            dma((2, nz)), dma((2, nz)), dma((2, nx)), dma((2, nx)), dma((2,)), dma((2,)),
        ],
        compiler_params=pltpu.CompilerParams(
            collective_id=0, has_side_effects=True, vmem_limit_bytes=48 << 20
        ),
        name="whole",
    )(*(pltpu.with_memory_space_constraint(a, pltpu.HBM) for a in arrays))


def store_kernel(
    block_out, region_grad, slab,
    block_to, region_to, reduce_grad, group_grad, expand_grad, shortcut_grad, group, sems,
):
    pairs = [
        (region_grad, region_to),
        (block_out, block_to),
        (slab.at[:, 768:1280], expand_grad),
        (slab.at[:, 0:256], reduce_grad),
        (slab.at[:, 512:768], shortcut_grad),
        (group, group_grad),
    ]
    copies = [pltpu.make_async_copy(a, b, sems.at[n]) for n, (a, b) in enumerate(pairs)]
    for copy in copies[:-1]:
        copy.start()
    group[...] = slab[:, 256:400]
    copies[-1].start()
    for copy in copies:
        copy.wait()


def store(block_out, region_grad, slab):
    kw = slab.shape[0]
    shape = jax.ShapeDtypeStruct
    return pl.pallas_call(
        store_kernel,
        out_shape=(
            shape(block_out.shape, BF),
            shape(region_grad.shape, BF),
            *(shape((kw, n), F32) for n in (256, 144, 512, 256)),
        ),
        in_specs=[VMEM] * 3,
        out_specs=(pl.BlockSpec(memory_space=pltpu.HBM),) * 6,
        scratch_shapes=[pltpu.VMEM((kw, 144), F32), pltpu.SemaphoreType.DMA((6,))],
        compiler_params=pltpu.CompilerParams(vmem_limit_bytes=4 << 20),
        name="store",
    )(block_out, region_grad, slab)


def solution(mesh):
    nr, nc = mesh.shape["row"], mesh.shape["col"]

    def per_device(region, reduce_weight, group_weight, expand_weight, shortcut_weight, cotangent):
        block_out, region_grad, *grads = store(
            *whole(
                nr, nc, reduce_weight.T, group_weight.T, expand_weight.T, shortcut_weight.T,
                region, cotangent,
            )
        )
        return (block_out, region_grad, *(grad.T for grad in grads))

    weight = P(None, "col")
    tile = P("row", "col", None)
    return jax.shard_map(
        per_device,
        mesh=mesh,
        in_specs=(tile, weight, weight, weight, weight, tile),
        out_specs=(tile, tile, weight, weight, weight, weight),
        check_vma=False,
    )
```

time: 60.2 us -> 51.6 us (0.86)
  Pallas kernels: 56 us -> 50.8 us
  local copies, waits for them, and re-layouts: 3.32 us -> 0 us
    pallas_call x4 -> x2, Pallas kernels: 56 us -> 50.8 us  [the longest x1 50 us: whole(): pl.pallas_call(functools.partial(whole_kernel, nr, nc), out_shape=(shape(...]
    unnamed x6 -> x0, local copies, waits for them, and re-layouts: 2.48 us -> none
    concatenate x1 -> x0, local copies, waits for them, and re-layouts: 0.84 us -> none  [per_device(): jnp.concatenate([reduce_weight, shortcut_weight, expand_weight, group_wei...]
where the time goes in v4:
time: 51.6 us; the launch traced here: 51.5 us
  Pallas kernels  50.8 us (98%)
  between operations  0.64 us (1%)
    pallas_call x1, Pallas kernels, whole(): pl.pallas_call(functools.partial(whole_kernel, nr, nc), out_shape=(shape(...  50 us

profile of v4, /device:TPU:1, one launch (start us, length us, event | category | flops | bytes accessed | tf_op | source)
XLA Modules:
  0.0 51.5 jit_solution(11551428769906526669)
XLA Ops:
  0.6 50.0 %whole.1 = (bf16[8,16,512]{2,1,0:T(8,128)(2,1)S(1)}, bf16[16,32,256]{2,1,0:T(8,128)(2,1)S(1)}, f32[16,1280]{1,0:T(8,128)S(1)}) custom-call(bf16[16,256]{1,0:T(8,128)(2,1)} %bitcast.9, bf16[16,144]{1,0:T(8,128)(2,1)} %bitcast.10, bf16[16,512]{1,0:T(8,128)(2,1)} %bitcast.8, bf16[16,256]{1,0:T(8,128)(2,1)} %bitcast.11, bf16[16,32,256]{2,1,0:T(8,128)(2,1)} %region.1, ...), custom_call_target="tpu_custom_call" | custom-call | tf_op jit(solution)/shard_map/whole/pallas_call | solution.py:527
  50.7 0.8 %store.1 = (bf16[8,16,512]{2,1,0:T(8,128)(2,1)}, bf16[16,32,256]{2,1,0:T(8,128)(2,1)}, f32[16,256]{1,0:T(8,128)}, f32[16,144]{1,0:T(8,128)}, f32[16,512]{1,0:T(8,128)}, /*index=5*/f32[16,256]{1,0:T(8,128)}) custom-call(bf16[8,16,512]{2,1,0:T(8,128)(2,1)S(1)} %get-tuple-element.15.block_out, bf16[16,32,256]{2,1,0:T(8,128)(2,1)S(1)} %get-tuple-element.16.region_grad, ...), custom_call_target="tpu_custom_call" | custom-call | tf_op jit(solution)/shard_map/store/pallas_call | solution.py:610

commit v5 on v4

--- a/solution.py
+++ b/solution.py
@@ -101,7 +101,7 @@
     full, xp, c32, hid, sl1, bdt, h2, sl2, wt, wg, regv, cotv, image, lstrip, fstrip, top, bot, cbot, lft, rgt,
     gsot, g2ot, g1t, gs, gso, g2, g1, rg, gt, rc, send, land, s2, rz, rx,
     ls, zs, zr, us, ur, ds, dr_, fs, fr, cs, cr, hs, hr,
-    rcs, rcr, rys, ryr, rzs, rzr, rxs, rxr, rfs, rfr,
+    rcs, rcr, rys, ryr, rzs, rzr, rxs, rxr,
 ):
     nz, nx, nh = nc // NY, nr // 2, nc // NY // 2
     row, col = lax.axis_index("row"), lax.axis_index("col")
@@ -122,10 +122,12 @@
         greet(row, lax.rem(z + d, nz) * NY + y)
     greet(row, z * NY + y_up)
     greet(row, z * NY + y_down)
+    greet(row, z * NY + y_far)
     greet(partner, col)
     for d in range(1, nx):
-        greet(2 * lax.rem(x + d, nx) + core, col)
-    count = nz + 2 + nx - 1
+        greet(2 * lax.rem(x + d, nx), col)
+        greet(2 * lax.rem(x + d, nx) + 1, col)
+    count = nz + 3 + 2 * (nx - 1)
     for dr in (-1, 0, 1):
         for dc in (-1, 0, 1):
             if dr == 0 and dc == 0:
@@ -155,6 +157,8 @@
     image[...] = jnp.zeros_like(image)
     c32[...] = jnp.zeros_like(c32)
 
+    lpart = (pl.ds(8, 8), pl.ds(0, 16), pl.ds(0, 8))
+    fpart = (pl.ds(0, 1), pl.ds(0, 3), pl.ds(1, 2))
     plan = [
         (has_down, 1, 0, regv.at[15], top, 0),
         (has_up, -1, 0, regv.at[pl.ds(0, 2)], bot, 1),
@@ -163,8 +167,8 @@
     for k, (there, step) in enumerate(((has_down, 1), (None, 0), (has_up, -1))):
         right = has_right if there is None else has_right & there
         left = has_left if there is None else has_left & there
-        plan.append((right, step, 1, lstrip, lft.at[k], 3 + k))
-        plan.append((left, step, -1, fstrip, rgt.at[k], 6 + k))
+        plan.append((right, step, 1, lstrip.at[lpart[k]], lft.at[k, lpart[k]], 3 + k))
+        plan.append((left, step, -1, fstrip.at[fpart[k]], rgt.at[k, fpart[k]], 6 + k))
     above = {0: has_up, 1: has_down, 2: has_down}
     for k, there in enumerate((has_up, None, has_down)):
         above[3 + k] = has_left if there is None else has_left & there
@@ -189,19 +193,21 @@
             image[h, (r + 1) * PW + 1 : (r + 1) * PW + 33] = regv[r, :, side].astype(F32)
         lstrip[:, side] = image[h, pl.ds(PW + 32, 16, stride=PW), :].astype(BF)
         for q in range(2):
-            fstrip[0, :, 256 * q + 128 * h : 256 * q + 128 * h + 128] = image[
-                h, pl.ds(PW + 1 + q, 16, stride=PW), :
-            ].astype(BF)
+            for e in range(2):
+                fstrip[1 - e, :, 256 * q + 128 * h : 256 * q + 128 * h + 128] = image[
+                    h, pl.ds((8 * e + 1) * PW + 1 + q, 8, stride=PW), :
+                ].astype(BF)
     for h in range(4):
         side = slice(128 * h, 128 * h + 128)
         for i in range(8):
             c32[h, i * S : i * S + 16] = cotv[i, :, side].astype(F32)
-        first = c32[h, pl.ds(0, 8, stride=S), :]
-        fstrip[1, :, side] = jnp.concatenate([first, jnp.zeros_like(first)], axis=0).astype(BF)
+        fstrip[2, :, side] = c32[h, pl.ds(0, 8, stride=S), :].astype(BF)
 
     pl.semaphore_wait(barrier, count)
 
     order = [nz // 2] + [n for d in range(nz // 2 - 1, 0, -1) for n in (d, nz - d)]
+    late = order[:3]
+    relayed = [d for d in [0] + order[::-1] if d not in late]
     along_z, upward, downward, forward = {}, {}, {}, {}
     for d in order:
         copy = remote(
@@ -215,6 +221,9 @@
         here = full.at[lax.rem(z + nz - d, nz), y, :, lanes]
         upward[d] = remote(here, here, us.at[d], ur.at[d], row, z * NY + y_up)
         downward[d] = remote(here, here, ds.at[d], dr_.at[d], row, z * NY + y_down)
+        if d in late:
+            forward[d] = remote(here, here, fs.at[d], fr.at[d], row, z * NY + y_far)
+            forward[d].start()
         upward[d].start()
         downward[d].start()
 
@@ -247,12 +256,12 @@
     for d in nearest:
         b = lax.rem(z + nz - d, nz)
         upward[d].wait_recv()
-        if d % 2 == 0:
+        if d in relayed[::2]:
             here = full.at[b, y_down, :, lanes]
             forward[d] = remote(here, here, fs.at[d], fr.at[d], row, z * NY + y_up)
             forward[d].start()
         downward[d].wait_recv()
-        if d % 2 == 1:
+        if d in relayed[1::2]:
             here = full.at[b, y_up, :, lanes]
             forward[d] = remote(here, here, fs.at[d], fr.at[d], row, z * NY + y_down)
             forward[d].start()
@@ -271,23 +280,25 @@
         for r in range(2):
             image[h, (17 + r) * PW + 1 : (17 + r) * PW + 33] = bot[r, :, side].astype(F32)
         image[h, pl.ds(PW, 16, stride=PW), :] = lft[1, :, side].astype(F32)
-        image[h, 0:1] = lft[0, :, side].astype(F32)[15:16]
-        below = lft[2, :, side].astype(F32)
+        image[h, 0:1] = lft[0, 8:16, side].astype(F32)[7:8]
+        below = lft[2, 0:8, side].astype(F32)
         for r in range(2):
             image[h, (17 + r) * PW : (17 + r) * PW + 1] = below[r : r + 1]
         for q in range(2):
             side = slice(256 * q + 128 * h, 256 * q + 128 * h + 128)
-            image[h, pl.ds(PW + 33 + q, 16, stride=PW), :] = rgt[1, 0, :, side].astype(F32)
-            image[h, 33 + q : 34 + q] = rgt[0, 0, :, side].astype(F32)[15:16]
-            corner = rgt[2, 0, :, side].astype(F32)
+            for e in range(2):
+                low = (8 * e + 1) * PW + 33 + q
+                image[h, pl.ds(low, 8, stride=PW), :] = rgt[1, 1 - e, :, side].astype(F32)
+            image[h, 33 + q : 34 + q] = rgt[0, 0, :, side].astype(F32)[7:8]
+            corner = rgt[2, 1, :, side].astype(F32)
             for r in range(2):
                 low = (17 + r) * PW + 33 + q
                 image[h, low : low + 1] = corner[r : r + 1]
     for h in range(4):
         side = slice(128 * h, 128 * h + 128)
         c32[h, 8 * S : 8 * S + 16] = cbot[:, side].astype(F32)
-        c32[h, pl.ds(16, 8, stride=S), :] = rgt[1, 1, :, side].astype(F32)[0:8]
-        c32[h, 8 * S + 16 : 8 * S + 17] = rgt[2, 1, :, side].astype(F32)[0:1]
+        c32[h, pl.ds(16, 8, stride=S), :] = rgt[1, 2, :, side].astype(F32)
+        c32[h, 8 * S + 16 : 8 * S + 17] = rgt[2, 2, :, side].astype(F32)[0:1]
     for k in range(4):
         pr, pc = divmod(k, 2)
         for i in range(10):
@@ -310,7 +321,7 @@
     other = [pl.ds(pl.multiple_of(first + (1 - core) * wide, 128), wide) for first, wide in CHUNKS]
     chunks = (1, 0)
 
-    across, along_y, turn_z, along_x, final = {}, {}, {}, {}, {}
+    across, along_y, turn_z, along_x = {}, {}, {}, {}
 
     def start_across(q):
         for n, at in enumerate((y_far, y_up, y_down, y)):
@@ -484,25 +495,27 @@
         for d in range(1, nz):
             turn_z[q, d].wait_recv()
             term = term + rz[1, d, :, part].astype(F32)
-        rx[x, :, part] = term
+        rx[x, :, mine[q]] = term.astype(BF)
         for d in range(1, nx):
-            here = rx.at[x, :, part]
-            copy = remote(
-                here, here, rxs.at[q, d], rxr.at[q, d], 2 * lax.rem(x + d, nx) + core, col
-            )
-            copy.start()
-            along_x[q, d] = copy
-    for q in chunks:
-        part = LOCAL[q]
-        for d in range(1, nx):
-            along_x[q, d].wait_recv()
-        term = rx[0, :, part]
-        for n in range(1, nx):
-            term = term + rx[n, :, part]
-        out[:, mine[q]] = term
-        here = out.at[:, mine[q]]
-        final[q] = remote(here, here, rfs.at[q], rfr.at[q], partner, col)
-        final[q].start()
+            for e in range(2):
+                here = rx.at[x, :, mine[q]]
+                to = lax.rem(core + e, 2)
+                copy = remote(
+                    here, here, rxs.at[q, 2 * d + e], rxr.at[q, 2 * d + e],
+                    2 * lax.rem(x + d, nx) + to, col,
+                )
+                copy.start()
+                along_x[q, 2 * d + e] = copy
+        here = rx.at[x, :, mine[q]]
+        copy = remote(here, here, rxs.at[q, 1], rxr.at[q, 1], partner, col)
+        copy.start()
+        along_x[q, 1] = copy
+    for copy in along_x.values():
+        copy.wait_recv()
+    term = rx[0].astype(F32)
+    for n in range(1, nx):
+        term = term + rx[n].astype(F32)
+    out[...] = term
     for there, copy, n in halos:
 
         @pl.when(there)
@@ -514,8 +527,6 @@
     for group in (along_z, upward, downward, forward, across, along_y, turn_z, along_x):
         for copy in group.values():
             copy.wait_send()
-    for copy in final.values():
-        copy.wait()
 
 
 def whole(nr, nc, *arrays):
@@ -548,12 +559,12 @@
             pltpu.VMEM((8, 16, 512), BF),
             pltpu.VMEM((2, 20 * PW, 128), F32),
             pltpu.VMEM((16, 256), BF),
-            pltpu.VMEM((2, 16, 512), BF),
+            pltpu.VMEM((3, 8, 512), BF),
             pltpu.VMEM((32, 256), BF),
             pltpu.VMEM((2, 32, 256), BF),
             pltpu.VMEM((16, 512), BF),
             pltpu.VMEM((3, 16, 256), BF),
-            pltpu.VMEM((3, 2, 16, 512), BF),
+            pltpu.VMEM((3, 3, 8, 512), BF),
             pltpu.VMEM((512, MW), BF),
             pltpu.VMEM((512, MW), BF),
             pltpu.VMEM((4, 512, MW), BF),
@@ -568,13 +579,13 @@
             pltpu.VMEM((6, nz // 2, kw, HALF), BF),
             pltpu.VMEM((nz, kw, HALF), F32),
             pltpu.VMEM((2, nz, kw, HALF), BF),
-            pltpu.VMEM((nx, kw, HALF), F32),
+            pltpu.VMEM((nx, kw, LANES), BF),
             dma((6,)),
             dma((nz,)), dma((nz,)), dma((nz,)), dma((nz,)),
             dma((nz,)), dma((nz,)), dma((nz,)), dma((nz,)),
             dma((4,)), dma((4,)), dma((9,)), dma((9,)),
             dma((2, 4)), dma((2, 4)), dma((2, 6)), dma((2, 6)),
-            dma((2, nz)), dma((2, nz)), dma((2, nx)), dma((2, nx)), dma((2,)), dma((2,)),
+            dma((2, nz)), dma((2, nz)), dma((2, nr)), dma((2, nr)),
         ],
         compiler_params=pltpu.CompilerParams(
             collective_id=0, has_side_effects=True, vmem_limit_bytes=48 << 20

time: 51.6 us -> 49.9 us (0.967)
  Pallas kernels: 50.8 us -> 49.2 us
    pallas_call x1, Pallas kernels: 50 us -> 48.4 us  [whole(): pl.pallas_call(functools.partial(whole_kernel, nr, nc), out_shape=(shape(...]
where the time goes in v5:
time: 49.9 us; the launch traced here: 49.8 us
  Pallas kernels  49.2 us (99%)
  between operations  0.64 us (1%)
    pallas_call x1, Pallas kernels, whole(): pl.pallas_call(functools.partial(whole_kernel, nr, nc), out_shape=(shape(...  48.4 us

profile of v5, /device:TPU:1, one launch (start us, length us, event | category | flops | bytes accessed | tf_op | source)
XLA Modules:
  0.0 49.8 jit_solution(8794684790562268132)
XLA Ops:
  0.6 48.4 %whole.1 = (bf16[8,16,512]{2,1,0:T(8,128)(2,1)S(1)}, bf16[16,32,256]{2,1,0:T(8,128)(2,1)S(1)}, f32[16,1280]{1,0:T(8,128)S(1)}) custom-call(bf16[16,256]{1,0:T(8,128)(2,1)} %bitcast.9, bf16[16,144]{1,0:T(8,128)(2,1)} %bitcast.10, bf16[16,512]{1,0:T(8,128)(2,1)} %bitcast.8, bf16[16,256]{1,0:T(8,128)(2,1)} %bitcast.11, bf16[16,32,256]{2,1,0:T(8,128)(2,1)} %region.1, ...), custom_call_target="tpu_custom_call" | custom-call | tf_op jit(solution)/shard_map/whole/pallas_call | solution.py:538
  49.0 0.8 %store.1 = (bf16[8,16,512]{2,1,0:T(8,128)(2,1)}, bf16[16,32,256]{2,1,0:T(8,128)(2,1)}, f32[16,256]{1,0:T(8,128)}, f32[16,144]{1,0:T(8,128)}, f32[16,512]{1,0:T(8,128)}, /*index=5*/f32[16,256]{1,0:T(8,128)}) custom-call(bf16[8,16,512]{2,1,0:T(8,128)(2,1)S(1)} %get-tuple-element.15.block_out, bf16[16,32,256]{2,1,0:T(8,128)(2,1)S(1)} %get-tuple-element.16.region_grad, ...), custom_call_target="tpu_custom_call" | custom-call | tf_op jit(solution)/shard_map/store/pallas_call | solution.py:621

commit v6 on v5

--- a/solution.py
+++ b/solution.py
@@ -25,6 +25,7 @@
 
 NN = (((1,), (0,)), ((), ()))
 NT = (((1,), (1,)), ((), ()))
+TN = (((0,), (0,)), ((), ()))
 
 
 def mm(lhs, rhs, dims):
@@ -79,9 +80,6 @@
                 piece = jnp.where(lane == g, piece, 0.0).astype(BF)
                 low = v * 128 + g * 16
                 bdt[tap, t, low : low + 16, v * 128 : v * 128 + 128] = piece
-                bdt[tap, t, low : low + 16, (1 - v) * 128 : (1 - v) * 128 + 128] = jnp.zeros(
-                    (16, 128), BF
-                )
 
     for t in range(2):
         half = slice(256 * t, 256 * t + 256)
@@ -99,7 +97,7 @@
     nr, nc, w_reduce, w_group, w_expand, w_short, region, cot,
     block_out, region_grad, out,
     full, xp, c32, hid, sl1, bdt, h2, sl2, wt, wg, regv, cotv, image, lstrip, fstrip, top, bot, cbot, lft, rgt,
-    gsot, g2ot, g1t, gs, gso, g2, g1, rg, gt, rc, send, land, s2, rz, rx,
+    g2o, gs, gso, g2, g1, rg, gt, rc, send, land, s2, rz, rx,
     ls, zs, zr, us, ur, ds, dr_, fs, fr, cs, cr, hs, hr,
     rcs, rcr, rys, ryr, rzs, rzr, rxs, rxr,
 ):
@@ -155,6 +153,7 @@
         load.start()
     wt[:, 256:512] = jnp.zeros((wt.shape[0], 256), BF)
     image[...] = jnp.zeros_like(image)
+    bdt[...] = jnp.zeros_like(bdt)
     c32[...] = jnp.zeros_like(c32)
 
     lpart = (pl.ds(8, 8), pl.ds(0, 16), pl.ds(0, 8))
@@ -206,10 +205,11 @@
     pl.semaphore_wait(barrier, count)
 
     order = [nz // 2] + [n for d in range(nz // 2 - 1, 0, -1) for n in (d, nz - d)]
+    across_x = [nx // 2] + [n for d in range(nx // 2 - 1, 0, -1) for n in (d, nx - d)]
     late = order[:3]
     relayed = [d for d in [0] + order[::-1] if d not in late]
     along_z, upward, downward, forward = {}, {}, {}, {}
-    for d in order:
+    for d in order[::-1]:
         copy = remote(
             wt.at[:, lanes], full.at[z, y, :, lanes], zs.at[d], zr.at[d],
             row, lax.rem(z + d, nz) * NY + y,
@@ -387,23 +387,21 @@
         cots = jnp.concatenate([c32[2 * n], c32[2 * n + 1]], axis=1)
         grad = cots * (gate + act * (1.0 - gate))
         gs[:, half] = grad.astype(BF)
-        kept = jnp.where(own, grad[:MW], 0.0)
-        gso[:, half] = kept.astype(BF)
-        gsot[half, :] = jnp.transpose(kept).astype(BF)
+        gso[:, half] = jnp.where(own, grad[:MW], 0.0).astype(BF)
 
     for n in range(2):
         half = slice(256 * n, 256 * n + 256)
-        put(256 * n, slice(512, 768), mm(gsot[half, :], strided[:MW], NN))
+        put(256 * n, slice(512, 768), mm(gso[:, half], strided[:MW], TN))
         for m in range(2):
             cols = slice(256 * m, 256 * m + 256)
-            put(256 * n, slice(768 + 256 * m, 1024 + 256 * m), mm(gsot[half, :], h2[:MW, cols], NN))
+            put(256 * n, slice(768 + 256 * m, 1024 + 256 * m), mm(gso[:, half], h2[:MW, cols], TN))
     start_across(1)
 
     for t in range(2):
         half = slice(256 * t, 256 * t + 256)
         grad = mm(gs[...], w_e[:, 256 * t : 256 * t + 256], NN) * sl2[:, half]
         g2[:, half] = grad.astype(BF).astype(F32)
-        g2ot[half, :] = jnp.transpose(jnp.where(own, grad[:MW], 0.0)).astype(BF)
+        g2o[:, half] = jnp.where(own, grad[:MW], 0.0).astype(BF)
 
     lane = lax.broadcasted_iota(jnp.int32, (16, 128), 1) // GW
     for u in range(4):
@@ -411,7 +409,7 @@
         sums = [[jnp.zeros((16, 128), F32)] * 8, [jnp.zeros((16, 128), F32)] * 8]
         for tap in range(9):
             k, off = tap_source(tap)
-            outer = mm(g2ot[block, :], hid[k, off : off + MW, block].astype(BF), NN)
+            outer = mm(g2o[:, block], hid[k, off : off + MW, block].astype(BF), TN)
             for g in range(8):
                 piece = outer[g * 16 : g * 16 + 16]
                 turn = ((tap % 8 - g) * 16) % 128
@@ -440,14 +438,13 @@
                 spread = spread + mm(g2[off : off + MW, half].astype(BF), bdt[tap, t], NN)
             grad = jnp.where(own, spread * sl1[k, window : window + MW, half], 0.0)
             g1[k, :, half] = grad.astype(BF)
-            g1t[k, half, :] = jnp.transpose(grad).astype(BF)
     for n in range(2):
         half = slice(256 * n, 256 * n + 256)
         grad = jnp.zeros((256, 256), F32)
         for k in range(4):
             pr, pc = divmod(k, 2)
             window = (1 - pr) * S + (1 - pc)
-            grad = grad + mm(g1t[k, half, :], xp[k, window : window + MW].astype(BF), NN)
+            grad = grad + mm(g1[k, :, half], xp[k, window : window + MW].astype(BF), TN)
         put(256 * n, slice(0, 256), grad)
     start_across(0)
 
@@ -496,7 +493,7 @@
             turn_z[q, d].wait_recv()
             term = term + rz[1, d, :, part].astype(F32)
         rx[x, :, mine[q]] = term.astype(BF)
-        for d in range(1, nx):
+        for d in across_x:
             for e in range(2):
                 here = rx.at[x, :, mine[q]]
                 to = lax.rem(core + e, 2)
@@ -565,9 +562,7 @@
             pltpu.VMEM((16, 512), BF),
             pltpu.VMEM((3, 16, 256), BF),
             pltpu.VMEM((3, 3, 8, 512), BF),
-            pltpu.VMEM((512, MW), BF),
-            pltpu.VMEM((512, MW), BF),
-            pltpu.VMEM((4, 512, MW), BF),
+            pltpu.VMEM((MW, 512), BF),
             pltpu.VMEM((MO, 512), BF),
             pltpu.VMEM((MW, 512), BF),
             pltpu.VMEM((MO, 512), F32),

time: 49.9 us -> 48.1 us (0.964)
  Pallas kernels: 49.2 us -> 47.4 us
    pallas_call x1, Pallas kernels: 48.4 us -> 46.5 us  [whole(): pl.pallas_call(functools.partial(whole_kernel, nr, nc), out_shape=(shape(...]
where the time goes in v6:
time: 48.1 us; the launch traced here: 48 us
  Pallas kernels  47.4 us (99%)
  between operations  0.64 us (1%)
    pallas_call x1, Pallas kernels, whole(): pl.pallas_call(functools.partial(whole_kernel, nr, nc), out_shape=(shape(...  46.5 us

profile of v6, /device:TPU:1, one launch (start us, length us, event | category | flops | bytes accessed | tf_op | source)
XLA Modules:
  0.0 48.0 jit_solution(11908881250385886955)
XLA Ops:
  0.6 46.5 %whole.1 = (bf16[8,16,512]{2,1,0:T(8,128)(2,1)S(1)}, bf16[16,32,256]{2,1,0:T(8,128)(2,1)S(1)}, f32[16,1280]{1,0:T(8,128)S(1)}) custom-call(bf16[16,256]{1,0:T(8,128)(2,1)} %bitcast.9, bf16[16,144]{1,0:T(8,128)(2,1)} %bitcast.10, bf16[16,512]{1,0:T(8,128)(2,1)} %bitcast.8, bf16[16,256]{1,0:T(8,128)(2,1)} %bitcast.11, bf16[16,32,256]{2,1,0:T(8,128)(2,1)} %region.1, ...), custom_call_target="tpu_custom_call" | custom-call | tf_op jit(solution)/shard_map/whole/pallas_call | solution.py:535
  47.2 0.8 %store.1 = (bf16[8,16,512]{2,1,0:T(8,128)(2,1)}, bf16[16,32,256]{2,1,0:T(8,128)(2,1)}, f32[16,256]{1,0:T(8,128)}, f32[16,144]{1,0:T(8,128)}, f32[16,512]{1,0:T(8,128)}, /*index=5*/f32[16,256]{1,0:T(8,128)}) custom-call(bf16[8,16,512]{2,1,0:T(8,128)(2,1)S(1)} %get-tuple-element.15.block_out, bf16[16,32,256]{2,1,0:T(8,128)(2,1)S(1)} %get-tuple-element.16.region_grad, ...), custom_call_target="tpu_custom_call" | custom-call | tf_op jit(solution)/shard_map/store/pallas_call | solution.py:616

commit v7 on v6

--- a/solution.py
+++ b/solution.py
@@ -478,7 +478,7 @@
             s2[nh + k, :, part] = (
                 chip(q, nh + k, y) + land[2, k, :, part].astype(F32) + land[5, k, :, part].astype(F32)
             )
-        for d in order:
+        for d in order[::-1]:
             to = lax.rem(z + d, nz)
             rz[0, d, :, part] = s2[to, :, part].astype(BF)
             copy = remote(

time: 48.1 us -> 48.3 us (level)
  no operation moved by 1% of the time
where the time goes in v7:
time: 48.3 us; the launch traced here: 48.2 us
  Pallas kernels  47.5 us (98%)
  between operations  0.64 us (1%)
    pallas_call x1, Pallas kernels, whole(): pl.pallas_call(functools.partial(whole_kernel, nr, nc), out_shape=(shape(...  46.7 us

profile of v7, /device:TPU:1, one launch (start us, length us, event | category | flops | bytes accessed | tf_op | source)
XLA Modules:
  0.0 48.2 jit_solution(13233789852084520044)
XLA Ops:
  0.6 46.7 %whole.1 = (bf16[8,16,512]{2,1,0:T(8,128)(2,1)S(1)}, bf16[16,32,256]{2,1,0:T(8,128)(2,1)S(1)}, f32[16,1280]{1,0:T(8,128)S(1)}) custom-call(bf16[16,256]{1,0:T(8,128)(2,1)} %bitcast.9, bf16[16,144]{1,0:T(8,128)(2,1)} %bitcast.10, bf16[16,512]{1,0:T(8,128)(2,1)} %bitcast.8, bf16[16,256]{1,0:T(8,128)(2,1)} %bitcast.11, bf16[16,32,256]{2,1,0:T(8,128)(2,1)} %region.1, ...), custom_call_target="tpu_custom_call" | custom-call | tf_op jit(solution)/shard_map/whole/pallas_call | solution.py:535
  47.3 0.8 %store.1 = (bf16[8,16,512]{2,1,0:T(8,128)(2,1)}, bf16[16,32,256]{2,1,0:T(8,128)(2,1)}, f32[16,256]{1,0:T(8,128)}, f32[16,144]{1,0:T(8,128)}, f32[16,512]{1,0:T(8,128)}, /*index=5*/f32[16,256]{1,0:T(8,128)}) custom-call(bf16[8,16,512]{2,1,0:T(8,128)(2,1)S(1)} %get-tuple-element.15.block_out, bf16[16,32,256]{2,1,0:T(8,128)(2,1)S(1)} %get-tuple-element.16.region_grad, ...), custom_call_target="tpu_custom_call" | custom-call | tf_op jit(solution)/shard_map/store/pallas_call | solution.py:616
